TPU v7x, 128 devices: a whole 4x4x4 slice. The times are simulated.
128 devices in a mesh: lat: 8 (over y, core), lon: 16 (over x, z).
Axes of the slice: x: 4, y: 4, z: 4, core: 2. Of those that a mesh axis runs over, the one named last changes fastest.
Arguments:
- obs_pert: bfloat16 [8192, 128, 256], P(('lat', 'lon')), may hold values from -4 to 4
- obs_dep: bfloat16 [8192, 128], P(('lat', 'lon')), may hold values from -6 to 6
- valid_rows: int32 [8192], P(('lat', 'lon')), may hold values from 1 to 128
- local_lists: int32 [512, 24], P(('lat', 'lon')), may hold values from 0 to 8191, as said below
- state_mean: float32 [8, 262144], P(None, ('lat', 'lon')), may hold values from -6 to 6
- state_pert: bfloat16 [8, 262144, 256], P(None, ('lat', 'lon')), may hold values from -6 to 6
- interp_lists: int32 [8192, 4], P(('lat', 'lon')), may hold values from 0 to 511, as said below
- interp_coef: float32 [4, 262144], P(None, ('lat', 'lon')), may hold values from 0.1 to 0.6
Outputs:
- analysis: bfloat16 [8, 262144, 256], P(None, ('lat', 'lon'))
Inputs may be any that keep to these rules, and one draw needn't show every extreme that they name: `local_lists`: device i of lat+lon stores blocks i * 64 to (i + 1) * 64 - 1. Among the lists of the 4 domains of one device, at most 2 entries name blocks stored on any one device, and on every owner some device serves exactly 2. Entries may repeat. `interp_lists`: domain g is owned by device g // 4 of lat+lon. Every domain named for a tile of device (a, b) is owned by a device whose lat index differs from a by at most 1 and whose lon index differs from b by at most 1 modulo the lon axis's size.
All inputs are finite; a program needn't handle non-finite values.
Results may differ from a plain program's by a relative error of at most 0.003.
Values may be sent and summed in bfloat16 or wider, within the bound.
A program may use at most 256 MiB of HBM per device.

v0:
```python
import jax
import jax.numpy as jnp
from jax import lax
from jax.sharding import PartitionSpec as P

NS_ITERS = 4


def with_halo(block, sides, width, periodic):
    for axis, dim in sides:
        count = lax.axis_size(axis)
        forward = [(i, i + 1) for i in range(count - 1)]
        if periodic:
            forward.append((count - 1, 0))
        backward = [(target, source) for source, target in forward]
        low = lax.ppermute(
            lax.slice_in_dim(block, block.shape[dim] - width, None, axis=dim), axis, forward
        )
        high = lax.ppermute(lax.slice_in_dim(block, 0, width, axis=dim), axis, backward)
        block = jnp.concatenate([low, block, high], axis=dim)
    return block


def make_weights(gram, innov, members):
    identity = jnp.eye(members, dtype=jnp.float32)
    system = (members - 1.0) * identity + gram
    scale = jnp.sqrt(jnp.sum(system * system, axis=(-2, -1)))[..., None, None]
    approx = system / scale
    inverse_root = jnp.broadcast_to(identity, system.shape)
    for sweep in range(NS_ITERS):
        factor = 1.5 * identity - 0.5 * jnp.matmul(
            inverse_root, approx, precision=lax.Precision.HIGHEST
        )
        approx = jnp.matmul(approx, factor, precision=lax.Precision.HIGHEST)
        inverse_root = jnp.matmul(factor, inverse_root, precision=lax.Precision.HIGHEST)
    inner = jnp.matmul(inverse_root, innov[..., None], precision=lax.Precision.HIGHEST)
    mean_weight = jnp.matmul(inverse_root, inner, precision=lax.Precision.HIGHEST) / scale
    return (jnp.sqrt((members - 1.0) / scale) * inverse_root + mean_weight).astype(jnp.bfloat16)


def local(
    obs_pert, obs_dep, valid_rows, local_lists, state_mean, state_pert, interp_lists, interp_coef
):
    n_devices = lax.axis_size(("lat", "lon"))
    n_lon = lax.axis_size("lon")
    blocks_here, block_rows, members = obs_pert.shape
    keep = jnp.arange(block_rows)[None, :] < valid_rows[:, None]
    masked_pert = jnp.where(keep[:, :, None], obs_pert, jnp.zeros((), jnp.bfloat16))
    masked_dep = jnp.where(keep, obs_dep, jnp.zeros((), jnp.bfloat16))
    capacity = 2 * max(1, 64 // n_devices)
    domains_here, list_len = local_lists.shape
    entries = local_lists.reshape(-1)
    source = entries // blocks_here
    local_index = entries % blocks_here
    onehot = (source[:, None] == jnp.arange(n_devices, dtype=jnp.int32)[None, :]).astype(jnp.int32)
    earlier = jnp.cumsum(onehot, axis=0) - onehot
    slot = jnp.sum(earlier * onehot, axis=1)
    flat_slot = source * capacity + slot
    request = jnp.zeros((n_devices * capacity,), jnp.int32).at[flat_slot].set(local_index)
    asked = lax.all_to_all(
        request.reshape(n_devices, capacity),
        ("lat", "lon"),
        split_axis=0,
        concat_axis=0,
        tiled=True,
    ).reshape(-1)
    out_pert = masked_pert[asked].reshape(n_devices, capacity, block_rows, members)
    out_dep = masked_dep[asked].reshape(n_devices, capacity, block_rows)
    arrived = (
        lax.all_to_all(out_pert, ("lat", "lon"), split_axis=0, concat_axis=0, tiled=True),
        lax.all_to_all(out_dep, ("lat", "lon"), split_axis=0, concat_axis=0, tiled=True),
    )
    got_pert = (
        arrived[0]
        .reshape(-1, block_rows, members)[flat_slot]
        .reshape(domains_here, list_len, block_rows, members)
    )
    got_dep = (
        arrived[1].reshape(-1, block_rows)[flat_slot].reshape(domains_here, list_len, block_rows)
    )
    gram = jnp.einsum("dlri,dlrj->dij", got_pert, got_pert, preferred_element_type=jnp.float32)
    innov = jnp.einsum("dlri,dlr->di", got_pert, got_dep, preferred_element_type=jnp.float32)
    weights = make_weights(gram, innov, members)
    tiles_near = with_halo(weights[None, None], (("lon", 1),), 1, True)
    tiles_near = with_halo(tiles_near, (("lat", 0),), 1, False)
    flat_tiles = tiles_near.reshape(9 * domains_here, members, members)
    owner = interp_lists // domains_here
    within = interp_lists % domains_here
    lat_step = owner // n_lon - lax.axis_index("lat")
    lon_step = (owner % n_lon - lax.axis_index("lon") + 1) % n_lon - 1
    position = ((lat_step + 1) * 3 + lon_step + 1) * domains_here + within
    chosen = flat_tiles[position]
    levels, cols_here, _ = state_pert.shape
    tiles_here, n_interp = interp_lists.shape
    tile_cols = cols_here // tiles_here
    perturbed = state_pert.reshape(levels, tiles_here, tile_cols, members)
    coef_tiles = interp_coef.reshape(n_interp, tiles_here, tile_cols)
    total = state_mean.reshape(levels, tiles_here, tile_cols)[..., None]
    for corner in range(n_interp):
        product = jnp.einsum(
            "ltci,tij->ltcj", perturbed, chosen[:, corner], preferred_element_type=jnp.float32
        )
        total = total + coef_tiles[corner][None, :, :, None] * product
    return total.reshape(levels, cols_here, members).astype(jnp.bfloat16)


def solution(mesh):
    in_specs = (
        P(("lat", "lon"), None, None),
        P(("lat", "lon"), None),
        P(("lat", "lon")),
        P(("lat", "lon"), None),
        P(None, ("lat", "lon")),
        P(None, ("lat", "lon"), None),
        P(("lat", "lon"), None),
        P(None, ("lat", "lon")),
    )
    out_specs = P(None, ("lat", "lon"), None)
    return jax.shard_map(local, mesh=mesh, in_specs=in_specs, out_specs=out_specs, check_vma=False)
```

profile of v0, /device:TPU:1, one launch (start us, length us, event | category | flops | bytes accessed | tf_op | source)
XLA Modules:
  0.0 471.2 jit_solution(4969660402857432700)
XLA Ops:
  3.6 11.5 %all-to-all-start = ((s32[128,1,2]{2,1,0:T(1,128)}), s32[128,1,2]{2,1,0:T(1,128)S(1)}, u32[]{:S(2)}, u32[]{:S(2)}) async-start(s32[128,1,2]{2,1,0:T(1,128)} %bitcast.2), calls=%async_computation | async-start | bytes 131072 | tf_op jit(solution)/shard_map/all_to_all | solution.py:60
  16.7 7.9 %all-to-all-done = s32[128,1,2]{2,1,0:T(1,128)S(1)} async-done(((s32[128,1,2]{2,1,0:T(1,128)}), s32[128,1,2]{2,1,0:T(1,128)S(1)}, u32[]{:S(2)}, u32[]{:S(2)}) %all-to-all-start) | async-done | bytes 1056 | tf_op jit(solution)/shard_map/all_to_all | solution.py:60
  26.1 1.5 gather_fusion.2
  27.5 4.5 all-to-all-start.2
  32.1 5.2 %broadcast_select_fusion = bf16[64,128,256]{2,1,0:T(8,128)(2,1)} fusion(bf16[64,128,256]{2,1,0:T(8,128)(2,1)} %param.8, pred[64,128]{1,0:T(8,128)(4,1)S(1)} %iota_compare_fusion.2), kind=kLoop, calls=%fused_computation.24 | loop fusion | flops 2097152 | bytes 8396800 | tf_op jit(solution)/shard_map/jit(_where)/select_n | solution.py:48
  37.3 11.5 %gather_fusion = bf16[256,128,256]{2,1,0:T(8,128)(2,1)} fusion(bf16[64,128,256]{2,1,0:T(8,128)(2,1)} %broadcast_select_fusion, s32[1024]{0:T(1024)S(1)} %pad_clamp_fusion.2), kind=kCustom, calls=%fused_computation | custom fusion | bytes 33555456 | tf_op jit(solution)/shard_map/gather | solution.py:67
  48.8 10.2 %all-to-all-start.1 = ((bf16[128,2,128,256]{3,2,1,0:T(8,128)(2,1)}), bf16[128,2,128,256]{3,2,1,0:T(8,128)(2,1)}, u32[]{:S(2)}, u32[]{:S(2)}) async-start(bf16[128,2,128,256]{3,2,1,0:T(8,128)(2,1)} %bitcast.125), calls=%async_computation.1 | async-start | bytes 33554432 | tf_op jit(solution)/shard_map/all_to_all | solution.py:70
  59.8 236.2 %all-to-all-done.1 = bf16[128,2,128,256]{3,2,1,0:T(8,128)(2,1)} async-done(((bf16[128,2,128,256]{3,2,1,0:T(8,128)(2,1)}), bf16[128,2,128,256]{3,2,1,0:T(8,128)(2,1)}, u32[]{:S(2)}, u32[]{:S(2)}) %all-to-all-start.1) | async-done | bytes 16777248 | tf_op jit(solution)/shard_map/all_to_all | solution.py:70
  296.0 12.3 %gather_fusion.1 = bf16[96,128,256]{2,1,0:T(8,128)(2,1)} fusion(bf16[256,128,256]{2,1,0:T(8,128)(2,1)} %bitcast.5, s32[1024]{0:T(1024)S(1)} %pad_clamp_fusion.1), kind=kCustom, calls=%fused_computation.1 | custom fusion | bytes 12583296 | tf_op jit(solution)/shard_map/gather | solution.py:74
  308.3 6.9 %multiply_reduce_fusion = (f32[4]{0:T(128)S(1)}, f32[4,256,256]{2,1,0:T(8,128)S(1)}) fusion(bf16[4,24,128,256]{3,2,1,0:T(8,128)(2,1)} %bitcast.121, f32[256,256]{1,0:T(8,128)S(1)} %fusion.22), kind=kOutput, calls=%fused_computation.37 | convolution fusion | flops 1611399168 | bytes 7602192 | tf_op jit(solution)/shard_map/dlri,dlrj->dij/dot_general | solution.py:81
  324.6 1.3 fusion.50
  333.1 10.8 %collective-permute-done.1 = bf16[1,1,4,256,256]{4,3,2,1,0:T(8,128)(2,1)S(1)} collective-permute-done((bf16[1,1,4,256,256]{4,3,2,1,0:T(8,128)(2,1)S(1)}, bf16[1,1,4,256,256]{4,3,2,1,0:T(8,128)(2,1)S(1)}, u32[]{:S(2)}, u32[]{:S(2)}) %collective-permute-start.1) | collective-permute-done | bytes 524320 | tf_op jit(solution)/shard_map/ppermute | solution.py:19
  344.0 4.2 collective-permute-done
  348.1 1.3 pad_maximum_fusion.1
  349.4 4.0 collective-permute-start.3
  353.4 7.5 %collective-permute-start.2 = (bf16[1,3,4,256,256]{4,3,2,1,0:T(8,128)(2,1)}, bf16[1,3,4,256,256]{4,3,2,1,0:T(8,128)(2,1)}, u32[]{:S(2)}, u32[]{:S(2)}) collective-permute-start(bf16[1,3,4,256,256]{4,3,2,1,0:T(8,128)(2,1)} %pad_maximum_fusion.1), channel_id=1, source_target_pairs={{0,16},{16,32},{32,48},{48,64},{64,80},{80,96},{96,112},{1,17},{17... | collective-permute-start | bytes 4718600 | tf_op jit(solution)/shard_map/ppermute | solution.py:16
  363.5 13.8 %collective-permute-done.3 = bf16[1,3,4,256,256]{4,3,2,1,0:T(8,128)(2,1)S(1)} collective-permute-done((bf16[1,3,4,256,256]{4,3,2,1,0:T(8,128)(2,1)}, bf16[1,3,4,256,256]{4,3,2,1,0:T(8,128)(2,1)S(1)}, u32[]{:S(2)}, u32[]{:S(2)}) %collective-permute-start.3) | collective-permute-done | bytes 1572896 | tf_op jit(solution)/shard_map/ppermute | solution.py:19
  378.6 3.8 pad_maximum_fusion
  382.4 16.2 %gather_fusion.4 = bf16[256,256,256]{2,1,0:T(8,128)(2,1)} fusion(bf16[36,256,256]{2,1,0:T(8,128)(2,1)} %bitcast.116, s32[1024]{0:T(1024)S(1)} %pad_clamp_fusion), kind=kCustom, calls=%fused_computation.4 | custom fusion | bytes 67109888 | tf_op jit(solution)/shard_map/gather | solution.py:92
  398.6 12.9 %fusion.2 = f32[64,256,8,32]{1,3,2,0:T(8,128)} fusion(bf16[64,4,256,256]{3,2,1,0:T(8,128)(2,1)} %bitcast.117, bf16[8,64,32,256]{3,2,1,0:T(8,128)(2,1)} %bitcast.112), kind=kOutput, calls=%fused_computation.14 | convolution fusion | flops 2147483648 | bytes 33554432 | tf_op jit(solution)/shard_map/ltci,tij->ltcj/dot_general | solution.py:100
  411.4 12.8 %fusion.3 = f32[64,256,8,32]{1,3,2,0:T(8,128)} fusion(bf16[64,4,256,256]{3,2,1,0:T(8,128)(2,1)} %bitcast.118, bf16[8,64,32,256]{3,2,1,0:T(8,128)(2,1)} %bitcast.113), kind=kOutput, calls=%fused_computation.16 | convolution fusion | flops 2147483648 | bytes 33554432 | tf_op jit(solution)/shard_map/ltci,tij->ltcj/dot_general | solution.py:100
  424.2 12.9 %fusion.4 = f32[64,256,8,32]{1,3,2,0:T(8,128)} fusion(bf16[64,4,256,256]{3,2,1,0:T(8,128)(2,1)} %bitcast.119, bf16[8,64,32,256]{3,2,1,0:T(8,128)(2,1)} %bitcast.114), kind=kOutput, calls=%fused_computation.18 | convolution fusion | flops 2147483648 | bytes 33554432 | tf_op jit(solution)/shard_map/ltci,tij->ltcj/dot_general | solution.py:100
  437.1 25.7 %fusion = bf16[8,64,32,256]{3,2,0,1:T(8,128)(2,1)} fusion(f32[64,256,8,32]{1,3,2,0:T(8,128)} %fusion.2, f32[64,256,8,32]{1,3,2,0:T(8,128)} %fusion.3, f32[64,256,8,32]{1,3,2,0:T(8,128)} %fusion.4, f32[64,32]{1,0:T(8,128)S(1)} %mul.144, f32[64,32]{1,0:T(8,128)S(1)} %mul.140, f32[64,32]{1,0:T(8,128)S(1)} %mul.136, f32[64,32]{1,0:T(8,128)S(1)} %mul.117, ...), kind=kOutput, calls=%fused_computation.7 | convolution fusion | flops 2185232384 | bytes 75595776 | tf_op jit(solution)/shard_map/ltci,tij->ltcj/dot_general | solution.py:100
  462.8 8.2 %copy.39 = bf16[8,64,32,256]{3,2,1,0:T(8,128)(2,1)} copy(bf16[8,64,32,256]{3,2,0,1:T(8,128)(2,1)} %fusion) | data formatting | bytes 16777216 | tf_op jit(solution)/shard_map/convert_element_type | solution.py:104
  (65 shorter events, 27.5 us)
Async XLA Ops:
  3.6 21.0 %all-to-all-start = ((s32[128,1,2]{2,1,0:T(1,128)}), s32[128,1,2]{2,1,0:T(1,128)S(1)}, u32[]{:S(2)}, u32[]{:S(2)}) async-start(s32[128,1,2]{2,1,0:T(1,128)} %bitcast.2), calls=%async_computation | async-start | bytes 131072 | tf_op jit(solution)/shard_map/all_to_all | solution.py:60
  27.5 21.3 %all-to-all-start.2 = ((bf16[128,2,128]{2,1,0:T(2,128)(2,1)}), bf16[128,2,128]{2,1,0:T(2,128)(2,1)S(1)}, u32[]{:S(2)}, u32[]{:S(2)}) async-start(bf16[128,2,128]{2,1,0:T(2,128)(2,1)} %bitcast.9), calls=%async_computation.2 | async-start | bytes 131072 | tf_op jit(solution)/shard_map/all_to_all | solution.py:71
  48.8 247.2 %all-to-all-start.1 = ((bf16[128,2,128,256]{3,2,1,0:T(8,128)(2,1)}), bf16[128,2,128,256]{3,2,1,0:T(8,128)(2,1)}, u32[]{:S(2)}, u32[]{:S(2)}) async-start(bf16[128,2,128,256]{3,2,1,0:T(8,128)(2,1)} %bitcast.125), calls=%async_computation.1 | async-start | bytes 33554432 | tf_op jit(solution)/shard_map/all_to_all | solution.py:70
  319.9 6.0 %slice-start = ((s8[6291456]{0:T(1024)(128)(4,1)}), s8[4194304]{0:T(1024)(128)(4,1)S(1)}, s32[]{:S(2)}) async-start(s8[6291456]{0:T(1024)(128)(4,1)} %bitcast.122), calls=%async_computation.3 | async-start | bytes 8388608
  322.2 3.7 slice-start.1
  326.0 35.0 %copy-start.2 = (s32[64,4]{0,1:T(4,128)S(1)}, s32[64,4]{0,1:T(4,128)}, u32[]{:S(2)}) copy-start(s32[64,4]{0,1:T(4,128)} %param.14) | copy-start | bytes 3076
  326.0 35.2 %copy-start.1 = (f32[4,2048]{1,0:T(4,128)S(1)}, f32[4,2048]{1,0:T(4,128)}, u32[]{:S(2)}) copy-start(f32[4,2048]{1,0:T(4,128)} %param.15) | copy-start | bytes 98308
  326.9 34.7 %copy-start = (f32[8,2048]{1,0:T(8,128)S(1)}, f32[8,2048]{1,0:T(8,128)}, u32[]{:S(2)}) copy-start(f32[8,2048]{1,0:T(8,128)} %param.12) | copy-start | bytes 196612
  331.6 12.4 %collective-permute-start.1 = (bf16[1,1,4,256,256]{4,3,2,1,0:T(8,128)(2,1)S(1)}, bf16[1,1,4,256,256]{4,3,2,1,0:T(8,128)(2,1)S(1)}, u32[]{:S(2)}, u32[]{:S(2)}) collective-permute-start(bf16[1,1,4,256,256]{4,3,2,1,0:T(8,128)(2,1)S(1)} %fusion.16), channel_id=1, source_target_pairs={{1,0},{2,1},{3,2},{4,3},{5,4},{6,5},{7,6},{8,7},{9,8},{10,9},{11,1... | collective-permute-start | bytes 1572872 | tf_op jit(solution)/shard_map/ppermute | solution.py:19
  332.5 15.6 %collective-permute-start = (bf16[1,1,4,256,256]{4,3,2,1,0:T(8,128)(2,1)S(1)}, bf16[1,1,4,256,256]{4,3,2,1,0:T(8,128)(2,1)S(1)}, u32[]{:S(2)}, u32[]{:S(2)}) collective-permute-start(bf16[1,1,4,256,256]{4,3,2,1,0:T(8,128)(2,1)S(1)} %fusion.16), channel_id=1, source_target_pairs={{0,1},{1,2},{2,3},{3,4},{4,5},{5,6},{6,7},{7,8},{8,9},{9,10},{10,1... | collective-permute-start | bytes 1572872 | tf_op jit(solution)/shard_map/ppermute | solution.py:16
  349.4 27.9 %collective-permute-start.3 = (bf16[1,3,4,256,256]{4,3,2,1,0:T(8,128)(2,1)}, bf16[1,3,4,256,256]{4,3,2,1,0:T(8,128)(2,1)S(1)}, u32[]{:S(2)}, u32[]{:S(2)}) collective-permute-start(bf16[1,3,4,256,256]{4,3,2,1,0:T(8,128)(2,1)} %pad_maximum_fusion.1), channel_id=1, source_target_pairs={{16,0},{32,16},{48,32},{64,48},{80,64},{96,80},{112,96},{17,1},{33... | collective-permute-start | bytes 4718600 | tf_op jit(solution)/shard_map/ppermute | solution.py:19
  353.4 25.2 %collective-permute-start.2 = (bf16[1,3,4,256,256]{4,3,2,1,0:T(8,128)(2,1)}, bf16[1,3,4,256,256]{4,3,2,1,0:T(8,128)(2,1)}, u32[]{:S(2)}, u32[]{:S(2)}) collective-permute-start(bf16[1,3,4,256,256]{4,3,2,1,0:T(8,128)(2,1)} %pad_maximum_fusion.1), channel_id=1, source_target_pairs={{0,16},{16,32},{32,48},{48,64},{64,80},{80,96},{96,112},{1,17},{17... | collective-permute-start | bytes 4718600 | tf_op jit(solution)/shard_map/ppermute | solution.py:16
where the time goes:
time: 477 us; the launch traced here: 471 us
  waiting for transfers between devices  274 us (57%)
  matrix products  87 us (18%)
  local copies, waits for them, and re-layouts  56.7 us (12%)
  starting transfers between devices  39.3 us (8%)
  other arithmetic  13.5 us (3%)
    all_to_all x1, waiting for transfers between devices, local(): lax.all_to_all(out_pert, ('lat', 'lon'), split_axis=0, concat_axis=0, til...  236 us
    dot_general x4, matrix products, local(): jnp.einsum('ltci,tij->ltcj', perturbed, chosen[:, corner], preferred_elem...  64.2 us
    ppermute x2, waiting for transfers between devices, with_halo(): lax.ppermute(lax.slice_in_dim(block, 0, width, axis=dim), axis, backward)  24.6 us
    gather x1, local copies, waits for them, and re-layouts, local(): chosen = flat_tiles[position]  16.2 us
    gather x1, local copies, waits for them, and re-layouts, local(): arrived[0].reshape(-1, block_rows, members)[flat_slot]  12.3 us
    gather x1, local copies, waits for them, and re-layouts, local(): masked_pert[asked].reshape(n_devices, capacity, block_rows, members)  11.5 us
    all_to_all x1, starting transfers between devices, local(): lax.all_to_all(request.reshape(n_devices, capacity), ('lat', 'lon'), spli...  11.5 us
    all_to_all x1, starting transfers between devices, local(): lax.all_to_all(out_pert, ('lat', 'lon'), split_axis=0, concat_axis=0, til...  10.2 us
  transfers between devices with their start and end apart: 7, of which 6 were waited for; matrix products, arithmetic and copies ran while one was open for 5% of the time, Pallas kernels for 0%

commit v1 on v0

v1 whole, which is shorter than its diff:
```python
import functools

import jax
import jax.numpy as jnp
from jax import lax
from jax.experimental import pallas as pl
from jax.experimental.pallas import tpu as pltpu
from jax.sharding import PartitionSpec as P

NS_ITERS = 4
MESH = pl.DeviceIdType.MESH
BIG = 1 << 20
PARTS = ((96, jnp.bfloat16, "xyz"), (96, jnp.bfloat16, "yzx"), (64, jnp.bfloat16, "zxy"), (8, jnp.float32, "zxy"))


def coords():
    a = lax.axis_index("lat")
    b = lax.axis_index("lon")
    return {"y": a // 2, "c": a % 2, "x": b // 4, "z": b % 4}


def device(pos):
    return (pos["y"] * 2 + pos["c"], pos["x"] * 4 + pos["z"])


def shifted(pos, axis, step):
    size = 2 if axis == "c" else 4
    return device({**pos, axis: (pos[axis] + step) % size})


def greet(peers):
    barrier = pltpu.get_barrier_semaphore()
    for peer in peers:
        pl.semaphore_signal(barrier, inc=1, device_id=peer, device_id_type=MESH)
    pl.semaphore_wait(barrier, len(peers))


def lists_kernel(tile_ref, pert_ref, dep_ref, keys_ref, sib_tile_ref, sib_pert_ref, sib_dep_ref,
                 held, send_sem, recv_sem, sib_send, sib_recv):
    pos = coords()
    x, y, z = pos["x"], pos["y"], pos["z"]
    sibling = shifted(pos, "c", 1)
    greet([shifted(pos, axis, step) for axis in "zxy" for step in (1, 2, 3)] + [sibling])
    swaps = []
    for k, (src, dst) in enumerate(((pert_ref, sib_pert_ref), (dep_ref, sib_dep_ref), (tile_ref, sib_tile_ref))):
        swap = pltpu.make_async_remote_copy(
            src_ref=src, dst_ref=dst, send_sem=sib_send.at[k], recv_sem=sib_recv.at[k],
            device_id=sibling, device_id_type=MESH)
        swap.start()
        swaps.append(swap)
    held[y, x, z] = tile_ref[...]
    sent = []
    for phase, axis in enumerate("zxy"):
        view = held.at[y, x, z] if axis == "z" else (held.at[y, x] if axis == "x" else held.at[y])
        copies = []
        for step in (1, 2, 3):
            copy = pltpu.make_async_remote_copy(
                src_ref=view, dst_ref=view, send_sem=send_sem.at[phase, step - 1],
                recv_sem=recv_sem.at[phase, step - 1],
                device_id=shifted(pos, axis, step), device_id_type=MESH)
            copy.start()
            copies.append(copy)
        for copy in copies:
            copy.wait_recv()
        sent += copies
    me = device(pos)
    own = me[0] * 16 + me[1]
    other = sibling[0] * 16 + sibling[1]
    entry = held[...].reshape(64, 8, 128)
    lane = lax.broadcasted_iota(jnp.int32, (64, 8, 128), 2)
    row = lax.broadcasted_iota(jnp.int32, (64, 8, 128), 1)
    owner = entry >> 6
    local_index = entry & 63
    block = jnp.where(owner == own, local_index, local_index + 64)
    value = jnp.where(((owner == own) | (owner == other)) & (row < 4), lane * 128 + block, BIG)
    out = jnp.full((64, 8, 128), BIG, jnp.int32)
    for k in range(4):
        least = jnp.min(value, axis=2, keepdims=True)
        out = jnp.where(lane == k, least, out)
        value = jnp.where(value > least, value, BIG)
    keys_ref[...] = out
    for copy in sent:
        copy.wait_send()
    for swap in swaps:
        swap.wait()


def gather_lists(tile, pert, dep):
    any_spec = pl.BlockSpec(memory_space=pl.ANY)
    vmem = pl.BlockSpec(memory_space=pltpu.VMEM)
    return pl.pallas_call(
        lists_kernel,
        out_shape=(
            jax.ShapeDtypeStruct((64, 8, 128), jnp.int32),
            jax.ShapeDtypeStruct((8, 128), jnp.int32),
            jax.ShapeDtypeStruct(pert.shape, pert.dtype),
            jax.ShapeDtypeStruct(dep.shape, dep.dtype),
        ),
        in_specs=[vmem, any_spec, any_spec],
        out_specs=(vmem, vmem, any_spec, any_spec),
        scratch_shapes=[
            pltpu.VMEM((4, 4, 4, 8, 128), jnp.int32),
            pltpu.SemaphoreType.DMA((3, 3)),
            pltpu.SemaphoreType.DMA((3, 3)),
            pltpu.SemaphoreType.DMA((3,)),
            pltpu.SemaphoreType.DMA((3,)),
        ],
        compiler_params=pltpu.CompilerParams(collective_id=0, has_side_effects=True),
        name="lists",
    )(tile, pert, dep)


def gram_kernel(keys_ref, valid_ref, pert_ref, sib_ref, dep_ref, sib_dep_ref, out0, out1, out2, out3, blocks, deps, sems):
    step = pl.program_id(0)

    @pl.when(step == 0)
    def _():
        loads = [
            pltpu.make_async_copy(pert_ref, blocks.at[pl.ds(0, 64)], sems.at[0]),
            pltpu.make_async_copy(sib_ref, blocks.at[pl.ds(64, 64)], sems.at[1]),
        ]
        for load in loads:
            load.start()
        deps[pl.ds(0, 64)] = dep_ref[...].astype(jnp.float32)
        deps[pl.ds(64, 64)] = sib_dep_ref[...].astype(jnp.float32)
        for load in loads:
            load.wait()

    rows = lax.broadcasted_iota(jnp.int32, (128, 256), 0)
    tri_row = lax.broadcasted_iota(jnp.int32, (128, 128), 0)
    tri_col = lax.broadcasted_iota(jnp.int32, (128, 128), 1)

    def piece(block):
        count = valid_ref[block]
        held = blocks[block]
        held = jnp.where(rows < count, held, jnp.zeros((), jnp.bfloat16))
        left, right = held[:, :128], held[:, 128:]
        top = lax.dot_general(left, held, (((0,), (0,)), ((), ())), preferred_element_type=jnp.float32)
        g22 = lax.dot_general(right, right, (((0,), (0,)), ((), ())), preferred_element_type=jnp.float32)
        g11, g12 = top[:, :128], top[:, 128:]
        packed = jnp.where(tri_col >= tri_row, g11, g22)
        d1 = jnp.sum(jnp.where(tri_col == tri_row, g11, 0.0), axis=0, keepdims=True)
        d2 = jnp.sum(jnp.where(tri_col == tri_row, g22, 0.0), axis=0, keepdims=True)
        dep = jnp.broadcast_to(deps[pl.ds(block, 1), :], (8, 128)).astype(jnp.bfloat16)
        inn = jnp.dot(dep, held, preferred_element_type=jnp.float32)
        extra = jnp.concatenate([d1, d2, inn[:1, :128], inn[:1, 128:], jnp.zeros((4, 128), jnp.float32)], axis=0)
        return g12, packed, extra

    def put(zz, dom, g12, packed, extra, add):
        def merge(ref, index, value):
            if add:
                value = value + ref[index].astype(jnp.float32)
            ref[index] = value.astype(ref.dtype)
        merge(out0, (0, 0, zz, pl.ds(dom * 96, 96)), g12[:96])
        merge(out1, (0, zz, 0, pl.ds(dom * 96, 32)), g12[96:])
        merge(out1, (0, zz, 0, pl.ds(dom * 96 + 32, 64)), packed[:64])
        merge(out2, (zz, 0, 0, pl.ds(dom * 64, 64)), packed[64:])
        merge(out3, (zz, 0, 0, pl.ds(dom * 8, 8)), extra)

    for zz in range(4):
        xx, yy = step // 4, step % 4
        base = ((yy * 4 + xx) * 4 + zz) * 16
        for dom in range(4):
            first = keys_ref[base + dom * 4]

            @pl.when(first >= BIG)
            def _():
                out0[0, 0, zz, pl.ds(dom * 96, 96)] = jnp.zeros((96, 128), jnp.bfloat16)
                out1[0, zz, 0, pl.ds(dom * 96, 96)] = jnp.zeros((96, 128), jnp.bfloat16)
                out2[zz, 0, 0, pl.ds(dom * 64, 64)] = jnp.zeros((64, 128), jnp.bfloat16)
                out3[zz, 0, 0, pl.ds(dom * 8, 8)] = jnp.zeros((8, 128), jnp.float32)

    def body(server_dom, carry):
        zz, dom = server_dom // 4, server_dom % 4
        xx, yy = step // 4, step % 4
        base = ((yy * 4 + xx) * 4 + zz) * 16 + dom * 4

        @pl.when(keys_ref[base] < BIG)
        def _():
            put(zz, dom, *piece(keys_ref[base] % 128), add=False)
            for k in range(1, 4):
                @pl.when(keys_ref[base + k] < BIG)
                def _():
                    put(zz, dom, *piece(keys_ref[base + k] % 128), add=True)
        return carry

    lax.fori_loop(0, 16, body, 0)


def partial_grams(keys, valid, pert, sib_pert, dep, sib_dep):
    any_spec = pl.BlockSpec(memory_space=pl.ANY)
    full = pl.BlockSpec((64, 128), lambda i, *_: (0, 0))
    maps = (
        ((1, 1, 4), lambda i, *_: (i // 4, i % 4, 0, 0, 0)),
        ((1, 4, 1), lambda i, *_: (i % 4, 0, i // 4, 0, 0)),
        ((4, 1, 1), lambda i, *_: (0, i // 4, i % 4, 0, 0)),
        ((4, 1, 1), lambda i, *_: (0, i // 4, i % 4, 0, 0)),
    )
    return pl.pallas_call(
        gram_kernel,
        out_shape=tuple(jax.ShapeDtypeStruct((4, 4, 4, 4 * r, 128), t) for r, t, _ in PARTS),
        grid_spec=pltpu.PrefetchScalarGridSpec(
            num_scalar_prefetch=2,
            grid=(16,),
            in_specs=[any_spec, any_spec, full, full],
            out_specs=tuple(
                pl.BlockSpec(lead + (4 * r, 128), index) for (r, _, _), (lead, index) in zip(PARTS, maps)
            ),
            scratch_shapes=[
                pltpu.VMEM((128, 128, 256), jnp.bfloat16),
                pltpu.VMEM((128, 128), jnp.float32),
                pltpu.SemaphoreType.DMA((2,)),
            ],
        ),
        compiler_params=pltpu.CompilerParams(
            dimension_semantics=("arbitrary",), vmem_limit_bytes=40 << 20),
        name="grams",
    )(keys, valid, pert, sib_pert, dep, sib_dep)


def split(value):
    high = value.astype(jnp.bfloat16)
    return high, (value - high.astype(jnp.float32)).astype(jnp.bfloat16)


def product(left, right):
    (lh, ll), (rh, rl) = left, right
    dot = functools.partial(jnp.dot, preferred_element_type=jnp.float32)
    return dot(lh, rh) + (dot(lh, rl) + dot(ll, rh))


def weights_of(g12, packed, extra, members):
    half = members // 2
    row = lax.broadcasted_iota(jnp.int32, (half, half), 0)
    col = lax.broadcasted_iota(jnp.int32, (half, half), 1)
    turned = packed.T
    g11 = jnp.where(col > row, packed, turned)
    g22 = jnp.where(col < row, packed, turned)
    g11 = jnp.where(col == row, extra[0:1], g11)
    g22 = jnp.where(col == row, extra[1:2], g22)
    gram = jnp.concatenate(
        [jnp.concatenate([g11, g12], axis=1), jnp.concatenate([g12.T, g22], axis=1)], axis=0)
    wide_row = lax.broadcasted_iota(jnp.int32, (members, members), 0)
    wide_col = lax.broadcasted_iota(jnp.int32, (members, members), 1)
    identity = jnp.where(wide_row == wide_col, 1.0, 0.0).astype(jnp.float32)
    system = (members - 1.0) * identity + gram
    total = jnp.sum(jnp.sum(system * system, axis=0, keepdims=True), axis=1, keepdims=True)
    scale = jnp.sqrt(total)
    approx = system / scale
    factor = 1.5 * identity - 0.5 * approx
    root = factor
    approx = product(split(approx), split(factor))
    for sweep in range(1, NS_ITERS):
        root_parts = split(root)
        factor = 1.5 * identity - 0.5 * product(root_parts, split(approx))
        factor_parts = split(factor)
        if sweep < NS_ITERS - 1:
            approx = product(split(approx), factor_parts)
        root = product(factor_parts, root_parts)
    innov = jnp.concatenate([extra[2:3], extra[3:4]], axis=1)
    innov = jnp.broadcast_to(innov, (8, members))
    root_parts = split(root)
    inner = product(split(innov), root_parts)
    mean = product(split(inner), root_parts) / scale
    mean_cols = jnp.concatenate(
        [jnp.broadcast_to(mean[:1, :half], (half, half)).T, jnp.broadcast_to(mean[:1, half:], (half, half)).T], axis=0)
    mean_full = jnp.concatenate([mean_cols, mean_cols], axis=1)
    return (jnp.sqrt((members - 1.0) / scale) * root + mean_full).astype(jnp.bfloat16)


def reduce_kernel(p0, p1, p2, p3, near_ref, *scratch):
    n = len(PARTS)
    parts = (p0, p1, p2, p3)
    scratch = list(scratch)

    def take(count):
        taken, scratch[:count] = scratch[:count], []
        return taken
    acc = take(n)
    side_r, side_l = take(n), take(n)
    bufs = [[take(6) for _ in range(n)] for _ in range(3)]
    fins = take(n)
    own, send_sem, recv_sem, load_sem, halo_send, halo_recv, own_sem = scratch

    pos = coords()
    a, b = lax.axis_index("lat"), lax.axis_index("lon")
    lat_up, lat_down = ((a + 1) % 8, b), ((a + 7) % 8, b)
    lon_up, lon_down = (a, (b + 1) % 16), (a, (b + 15) % 16)
    loads = []
    for i, (_, _, order) in enumerate(PARTS):
        m = pos[order[0]]
        mine = [
            pltpu.make_async_copy(parts[i].at[(m + 1) % 4, pl.ds(0, 2)], side_r[i], load_sem.at[i, 0]),
            pltpu.make_async_copy(parts[i].at[(m + 3) % 4, pl.ds(2, 2)], side_l[i], load_sem.at[i, 1]),
            pltpu.make_async_copy(parts[i].at[m], acc[i], load_sem.at[i, 2]),
        ]
        for load in mine:
            load.start()
        loads.append(mine)
    greet([shifted(pos, axis, step) for axis in "xyz" for step in (1, 3)] + [lat_up, lat_down, lon_up, lon_down])

    sends = []

    def slab(i, phase, target, upper):
        rows = PARTS[i][0]
        order = PARTS[i][2]
        if phase == 0:
            return parts[i].at[target, pl.ds(2 * upper, 2)]
        if phase == 1:
            return acc[i].at[target, pl.ds(2 * upper, 2)]
        return acc[i].at[pos[order[1]], target, pl.ds(2 * rows * upper, 2 * rows)]

    for phase in range(3):
        def start(i, k, source, to_right):
            axis = PARTS[i][2][phase]
            copy = pltpu.make_async_remote_copy(
                src_ref=source, dst_ref=bufs[phase][i][k],
                send_sem=send_sem.at[phase, i, k], recv_sem=recv_sem.at[phase, i, k],
                device_id=shifted(pos, axis, 1 if to_right else 3), device_id_type=MESH)
            copy.start()
            sends.append(copy)
            return copy

        flights = [[None] * 6 for _ in range(n)]
        for i in range(n):
            m = pos[PARTS[i][2][phase]]
            flights[i][0] = start(i, 0, slab(i, phase, (m + 2) % 4, 0), True)
            flights[i][1] = start(i, 1, slab(i, phase, (m + 2) % 4, 1), False)
        for i in range(n):
            m = pos[PARTS[i][2][phase]]
            flights[i][2] = start(i, 2, slab(i, phase, (m + 1) % 4, 1), True)
            flights[i][3] = start(i, 3, slab(i, phase, (m + 3) % 4, 0), False)
        for i in range(n):
            rows, dtype, order = PARTS[i]
            m = pos[order[phase]]
            for k, (target, upper) in enumerate((((m + 1) % 4, 0), ((m + 3) % 4, 1))):
                flights[i][k].wait_recv()
                got = bufs[phase][i][k]
                if phase == 0:
                    loads[i][k].wait()
                    side = (side_r, side_l)[k][i]

                    def body(j, carry, got=got, side=side):
                        p, q = j // 4, j % 4
                        got[p, q] = (got[p, q].astype(jnp.float32) + side[p, q].astype(jnp.float32)).astype(got.dtype)
                        return carry
                    lax.fori_loop(0, 8, body, 0)
                elif phase == 1:
                    def body(j, carry, got=got, target=target, upper=upper, i=i):
                        got[j] = (got[j].astype(jnp.float32)
                                  + acc[i][target, 2 * upper + j].astype(jnp.float32)).astype(got.dtype)
                        return carry
                    lax.fori_loop(0, 2, body, 0)
                else:
                    mine = acc[i][pos[order[1]], target, pl.ds(2 * rows * upper, 2 * rows)]
                    got[...] = (got[...].astype(jnp.float32) + mine.astype(jnp.float32)).astype(got.dtype)
                flights[i][4 + k] = start(i, 4 + k, got, k == 0)
        for i in range(n):
            rows, dtype, order = PARTS[i]
            m = pos[order[phase]]
            for k in (2, 3, 4, 5):
                flights[i][k].wait_recv()
            buf = bufs[phase][i]
            pairs = ((4, 3), (2, 5))
            if phase == 0:
                loads[i][2].wait()
            for upper, (k0, k1) in enumerate(pairs):
                f, g = buf[k0], buf[k1]
                if phase == 0:
                    def body(j, carry, f=f, g=g, upper=upper, i=i):
                        p, q = j // 4, j % 4
                        total = (acc[i][2 * upper + p, q].astype(jnp.float32) + f[p, q].astype(jnp.float32)
                                 + g[p, q].astype(jnp.float32))
                        acc[i][2 * upper + p, q] = total.astype(acc[i].dtype)
                        return carry
                    lax.fori_loop(0, 8, body, 0)
                elif phase == 1:
                    def body(j, carry, f=f, g=g, upper=upper, i=i, m=m):
                        total = (acc[i][m, 2 * upper + j].astype(jnp.float32) + f[j].astype(jnp.float32)
                                 + g[j].astype(jnp.float32))
                        acc[i][m, 2 * upper + j] = total.astype(acc[i].dtype)
                        return carry
                    lax.fori_loop(0, 2, body, 0)
                else:
                    span = pl.ds(2 * rows * upper, 2 * rows)
                    fins[i][span] = (acc[i][pos[order[1]], m, span].astype(jnp.float32)
                                     + f[...].astype(jnp.float32) + g[...].astype(jnp.float32))

    def solve(d, carry):
        g12 = jnp.concatenate([fins[0][pl.ds(d * 96, 96)], fins[1][pl.ds(d * 96, 32)]], axis=0)
        packed = jnp.concatenate([fins[1][pl.ds(d * 96 + 32, 64)], fins[2][pl.ds(d * 64, 64)]], axis=0)
        own[d] = weights_of(g12, packed, fins[3][pl.ds(d * 8, 8)], 256)
        return carry
    lax.fori_loop(0, 4, solve, 0)

    keep = pltpu.make_async_copy(own, near_ref.at[1, 1], own_sem)
    keep.start()

    def halo(k, source, dst, target):
        copy = pltpu.make_async_remote_copy(
            src_ref=source, dst_ref=dst, send_sem=halo_send.at[k], recv_sem=halo_recv.at[k],
            device_id=target, device_id_type=MESH)
        copy.start()
        sends.append(copy)
        return copy
    east = halo(0, own, near_ref.at[1, 0], lon_up)
    west = halo(1, own, near_ref.at[1, 2], lon_down)
    arriving = [halo(2, own, near_ref.at[0, 1], lat_up), halo(3, own, near_ref.at[2, 1], lat_down)]
    east.wait_recv()
    arriving += [halo(4, near_ref.at[1, 0], near_ref.at[0, 0], lat_up),
                 halo(5, near_ref.at[1, 0], near_ref.at[2, 0], lat_down)]
    west.wait_recv()
    arriving += [halo(6, near_ref.at[1, 2], near_ref.at[0, 2], lat_up),
                 halo(7, near_ref.at[1, 2], near_ref.at[2, 2], lat_down)]
    for copy in arriving:
        copy.wait_recv()
    for copy in sends:
        copy.wait_send()
    keep.wait()


def near_weights(parts):
    n = len(PARTS)
    any_spec = pl.BlockSpec(memory_space=pl.ANY)
    def vmem(shape, kind):
        return pltpu.VMEM(shape, kind)
    scratch = [vmem((4, 4, 4 * r, 128), t) for r, t, _ in PARTS]
    scratch += [vmem((2, 4, 4 * r, 128), t) for r, t, _ in PARTS] * 2
    for phase in range(3):
        for r, t, _ in PARTS:
            shape = ((2, 4, 4 * r, 128), (2, 4 * r, 128), (2 * r, 128))[phase]
            scratch += [vmem(shape, t)] * 6
    scratch += [vmem((4 * r, 128), jnp.float32) for r, _, _ in PARTS]
    scratch += [
        vmem((4, 256, 256), jnp.bfloat16),
        pltpu.SemaphoreType.DMA((3, n, 6)),
        pltpu.SemaphoreType.DMA((3, n, 6)),
        pltpu.SemaphoreType.DMA((n, 3)),
        pltpu.SemaphoreType.DMA((8,)),
        pltpu.SemaphoreType.DMA((8,)),
        pltpu.SemaphoreType.DMA(()),
    ]
    return pl.pallas_call(
        reduce_kernel,
        out_shape=jax.ShapeDtypeStruct((3, 3, 4, 256, 256), jnp.bfloat16),
        in_specs=[any_spec] * n,
        out_specs=any_spec,
        scratch_shapes=scratch,
        compiler_params=pltpu.CompilerParams(
            collective_id=1, has_side_effects=True, vmem_limit_bytes=52 << 20),
        name="reduce",
    )(*parts)


STEP_TILES = 4


def interp_kernel(pos_ref, pert_ref, mean_ref, coef_ref, near_ref, out_ref):
    step = pl.program_id(0)
    mean_cols = mean_ref[...].T
    coef = coef_ref[...]
    coef_cols = jnp.concatenate([coef, coef], axis=0).T
    for tile in range(STEP_TILES):
        span = pl.ds(tile * 32, 32)
        held = pert_ref[:, span, :].reshape(256, 256)
        total = None
        for corner in range(4):
            where = pos_ref[(step * STEP_TILES + tile) * 4 + corner]
            prod = jnp.dot(held, near_ref[where], preferred_element_type=jnp.float32)
            factor = coef_cols[tile * 32:tile * 32 + 32, corner:corner + 1]
            term = prod.reshape(8, 32, 256) * factor[None]
            total = term if total is None else total + term
        for level in range(8):
            base = mean_cols[tile * 32:tile * 32 + 32, level:level + 1]
            out_ref[level, span, :] = (total[level] + base).astype(jnp.bfloat16)


def interpolate(position, pert, mean, coef, near):
    cols = STEP_TILES * 32
    steps = pert.shape[1] // cols
    return pl.pallas_call(
        interp_kernel,
        out_shape=jax.ShapeDtypeStruct(pert.shape, jnp.bfloat16),
        grid_spec=pltpu.PrefetchScalarGridSpec(
            num_scalar_prefetch=1,
            grid=(steps,),
            in_specs=[
                pl.BlockSpec((8, cols, 256), lambda i, *_: (0, i, 0)),
                pl.BlockSpec((8, cols), lambda i, *_: (0, i)),
                pl.BlockSpec((4, cols), lambda i, *_: (0, i)),
                pl.BlockSpec((36, 256, 256), lambda i, *_: (0, 0, 0), pipeline_mode=pl.Buffered(1)),
            ],
            out_specs=pl.BlockSpec((8, cols, 256), lambda i, *_: (0, i, 0)),
        ),
        compiler_params=pltpu.CompilerParams(
            dimension_semantics=("arbitrary",), vmem_limit_bytes=32 << 20),
        name="interp",
    )(position, pert, mean, coef, near)


def local(
    obs_pert, obs_dep, valid_rows, local_lists, state_mean, state_pert, interp_lists, interp_coef
):
    n_lon = lax.axis_size("lon")
    domains_here = local_lists.shape[0]
    tile = jnp.concatenate([
        jnp.pad(local_lists, ((0, 0), (0, 128 - local_lists.shape[1])), constant_values=-1),
        jnp.pad(valid_rows[None, :], ((0, 3), (0, 64))),
    ], axis=0)
    keys, sib_tile, sib_pert, sib_dep = gather_lists(tile, obs_pert, obs_dep)
    keys = keys[:, :4, :4].reshape(-1)
    valid = jnp.concatenate([valid_rows, sib_tile[4, :64]])
    parts = partial_grams(keys, valid, obs_pert, sib_pert, obs_dep, sib_dep)
    near = near_weights(parts)
    owner = interp_lists // domains_here
    within = interp_lists % domains_here
    lat_step = owner // n_lon - lax.axis_index("lat")
    lon_step = (owner % n_lon - lax.axis_index("lon") + 1) % n_lon - 1
    position = ((lat_step + 1) * 3 + lon_step + 1) * domains_here + within
    return interpolate(position.reshape(-1), state_pert, state_mean, interp_coef, near.reshape(36, 256, 256))


def solution(mesh):
    in_specs = (
        P(("lat", "lon"), None, None),
        P(("lat", "lon"), None),
        P(("lat", "lon")),
        P(("lat", "lon"), None),
        P(None, ("lat", "lon")),
        P(None, ("lat", "lon"), None),
        P(("lat", "lon"), None),
        P(None, ("lat", "lon")),
    )
    out_specs = P(None, ("lat", "lon"), None)
    return jax.shard_map(local, mesh=mesh, in_specs=in_specs, out_specs=out_specs, check_vma=False)
```

time: 477 us -> 211 us (0.44); the launches traced: 471 us -> 211 us
  waiting for transfers between devices: 274 us -> 0 us
  Pallas kernels: 0 us -> 193 us
  matrix products: 87 us -> 0 us
  local copies, waits for them, and re-layouts: 56.7 us -> 15.6 us
  starting transfers between devices: 39.3 us -> 0 us
  other arithmetic: 13.5 us -> 2.06 us
    all_to_all x3 -> x0, waiting for transfers between devices: 244 us -> none  [the longest x1 236 us: local(): lax.all_to_all(out_pert, ('lat', 'lon'), split_axis=0, concat_axis=0, til...]
    pallas_call x0 -> x4, Pallas kernels: none -> 193 us  [the longest x1 127 us: near_weights(): pl.pallas_call(reduce_kernel, out_shape=jax.ShapeDtypeStruct((3, 3, 4, 25...]
    dot_general x19 -> x0, matrix products: 87 us -> none  [the longest x4 64.2 us: local(): jnp.einsum('ltci,tij->ltcj', perturbed, chosen[:, corner], preferred_elem...]
    gather x5 -> x0, local copies, waits for them, and re-layouts: 42.1 us -> none  [the longest x1 16.2 us: local(): chosen = flat_tiles[position]]
    ppermute x4 -> x0, waiting for transfers between devices: 30.1 us -> none  [the longest x2 24.6 us: with_halo(): lax.ppermute(lax.slice_in_dim(block, 0, width, axis=dim), axis, backward)]
    all_to_all x3 -> x0, starting transfers between devices: 26.2 us -> none  [the longest x1 11.5 us: local(): lax.all_to_all(request.reshape(n_devices, capacity), ('lat', 'lon'), spli...]
    unnamed x10 -> x20, local copies, waits for them, and re-layouts: 0.03 us -> 13.6 us
    ppermute x4 -> x0, starting transfers between devices: 13 us -> none  [the longest x2 8.1 us: with_halo(): lax.ppermute(lax.slice_in_dim(block, block.shape[dim] - width, None, axis...]
  transfers between devices with their start and end apart: 7 -> 0, of which waited for: 6 -> 0; matrix products, arithmetic and copies ran while one was open for 5% -> 0% of each run, Pallas kernels for 0% -> 0%
where the time goes in v1:
time: 211 us
  Pallas kernels  193 us (91%)
  local copies, waits for them, and re-layouts  15.6 us (7%)
    pallas_call x1, Pallas kernels, near_weights(): pl.pallas_call(reduce_kernel, out_shape=jax.ShapeDtypeStruct((3, 3, 4, 25...  127 us
    pallas_call x1, Pallas kernels, partial_grams(): pl.pallas_call(gram_kernel, out_shape=tuple((jax.ShapeDtypeStruct((4, 4,...  33 us
    pallas_call x1, Pallas kernels, gather_lists(): pl.pallas_call(lists_kernel, out_shape=(jax.ShapeDtypeStruct((64, 8, 128)...  18.6 us
    pallas_call x1, Pallas kernels, interpolate(): pl.pallas_call(interp_kernel, out_shape=jax.ShapeDtypeStruct(pert.shape,...  14.3 us
    unnamed x20, local copies, waits for them, and re-layouts  13.6 us

profile of v1, /device:TPU:1, one launch (start us, length us, event | category | flops | bytes accessed | tf_op | source)
XLA Modules:
  0.0 210.6 jit_solution(2669737561059154105)
XLA Ops:
  0.0 1.3 pad_add_fusion.tile_ref
  1.3 18.6 %lists.1 = (s32[64,8,128]{2,1,0:T(8,128)}, s32[8,128]{1,0:T(8,128)}, bf16[64,128,256]{2,1,0:T(8,128)(2,1)}, bf16[64,128]{1,0:T(8,128)(2,1)}) custom-call(s32[8,128]{1,0:T(8,128)} %pad_add_fusion.tile_ref, bf16[64,128,256]{2,1,0:T(8,128)(2,1)} %pert_ref.4, bf16[64,128]{1,0:T(8,128)(2,1)} %dep_ref.3), custom_call_target="tpu_custom_call" | custom-call | tf_op jit(solution)/shard_map/lists/pallas_call | solution.py:91
  19.9 1.0 slice.6
  20.9 0.2 reshape.10.keys_ref
  21.0 0.7 slice_bitcast_fusion
  21.7 0.7 pad_add_fusion.1.valid_ref
  22.4 0.0 copy-start.1
  22.4 2.2 %copy-done.1 = bf16[64,128,256]{2,1,0:T(8,128)(2,1)S(1)} copy-done((bf16[64,128,256]{2,1,0:T(8,128)(2,1)S(1)}, bf16[64,128,256]{2,1,0:T(8,128)(2,1)}, u32[]{:S(2)}) %copy-start.1) | copy-done | bytes 4194328
  24.6 2.2 %copy-done.3 = bf16[64,128,256]{2,1,0:T(8,128)(2,1)S(1)} copy-done((bf16[64,128,256]{2,1,0:T(8,128)(2,1)S(1)}, bf16[64,128,256]{2,1,0:T(8,128)(2,1)}, u32[]{:S(2)}) %copy-start.3) | copy-done | bytes 4194328
  26.8 0.7 copy-done.6
  27.5 0.7 copy-done.8
  28.3 33.0 %grams.1 = (bf16[4,4,4,384,128]{4,3,2,1,0:T(8,128)(2,1)}, bf16[4,4,4,384,128]{4,3,2,1,0:T(8,128)(2,1)}, bf16[4,4,4,256,128]{4,3,2,1,0:T(8,128)(2,1)S(1)}, f32[4,4,4,32,128]{4,3,2,1,0:T(8,128)S(1)}) custom-call(s32[1024]{0:T(1024)S(1)} %reshape.10.keys_ref, s32[128]{0:T(128)S(1)} %pad_add_fusion.1.valid_ref, bf16[64,128,256]{2,1,0:T(8,128)(2,1)S(1)} %copy-done.1, ...), custom_call_target="tpu_custom_call" | custom-call | tf_op jit(solution)/shard_map/grams/pallas_call | solution.py:199
  61.3 0.0 copy-start.4
  61.3 2.0 copy-done.4
  63.3 127.0 %reduce.1 = bf16[3,3,4,256,256]{4,3,2,1,0:T(8,128)(2,1)} custom-call(bf16[4,4,4,384,128]{4,3,2,1,0:T(8,128)(2,1)} %get-tuple-element.17.p0, bf16[4,4,4,384,128]{4,3,2,1,0:T(8,128)(2,1)} %get-tuple-element.18.p1, bf16[4,4,4,256,128]{4,3,2,1,0:T(8,128)(2,1)} %copy-done.4, f32[4,4,4,32,128]{4,3,2,1,0:T(8,128)S(1)} %get-tuple-element.20.p3), custom_call_target="tpu_custom_call" | custom-call | tf_op jit(solution)/shard_map/reduce/pallas_call | solution.py:443
  190.4 0.0 copy-done.9
  190.4 0.1 copy.9
  190.5 0.1 reshape.9.pos_ref
  190.6 0.0 copy-done.5
  190.6 0.0 copy-done.7
  190.6 0.0 copy-start
  190.6 2.3 %copy-done = bf16[3,3,4,256,256]{4,3,2,1,0:T(8,128)(2,1)S(1)} copy-done((bf16[3,3,4,256,256]{4,3,2,1,0:T(8,128)(2,1)S(1)}, bf16[3,3,4,256,256]{4,3,2,1,0:T(8,128)(2,1)}, u32[]{:S(2)}) %copy-start) | copy-done | bytes 4718616
  193.0 3.4 %copy-done.2 = bf16[8,2048,256]{2,1,0:T(8,128)(2,1)S(1)} copy-done((bf16[8,2048,256]{2,1,0:T(8,128)(2,1)S(1)}, bf16[8,2048,256]{2,1,0:T(8,128)(2,1)}, u32[]{:S(2)}) %copy-start.2) | copy-done | bytes 8388632
  196.4 14.3 %interp.1 = bf16[8,2048,256]{2,1,0:T(8,128)(2,1)} custom-call(s32[256]{0:T(256)S(1)} %reshape.9.pos_ref, bf16[8,2048,256]{2,1,0:T(8,128)(2,1)S(1)} %copy-done.2, f32[8,2048]{1,0:T(8,128)S(1)} %copy-done.5, f32[4,2048]{1,0:T(4,128)S(1)} %copy-done.7, bf16[36,256,256]{2,1,0:T(8,128)(2,1)S(1)} %bitcast.4), custom_call_target="tpu_custom_call" | custom-call | tf_op jit(solution)/shard_map/interp/pallas_call | solution.py:481
  (8 shorter events, 0.0 us)
Async XLA Ops:
  22.4 2.2 %copy-start.1 = (bf16[64,128,256]{2,1,0:T(8,128)(2,1)S(1)}, bf16[64,128,256]{2,1,0:T(8,128)(2,1)}, u32[]{:S(2)}) copy-start(bf16[64,128,256]{2,1,0:T(8,128)(2,1)} %pert_ref.4) | copy-start | bytes 12582916
  24.6 2.2 %copy-start.3 = (bf16[64,128,256]{2,1,0:T(8,128)(2,1)S(1)}, bf16[64,128,256]{2,1,0:T(8,128)(2,1)}, u32[]{:S(2)}) copy-start(bf16[64,128,256]{2,1,0:T(8,128)(2,1)} %get-tuple-element.15.sib_ref) | copy-start | bytes 12582916
  26.8 0.7 copy-start.6
  27.5 0.7 copy-start.8
  61.3 2.1 copy-start.4
  63.3 127.1 %copy-start.9 = (s32[64,4]{0,1:T(4,128)S(1)}, s32[64,4]{0,1:T(4,128)}, u32[]{:S(2)}) copy-start(s32[64,4]{0,1:T(4,128)} %param.14) | copy-start | bytes 3076
  63.3 127.3 %copy-start.5 = (f32[8,2048]{1,0:T(8,128)S(1)}, f32[8,2048]{1,0:T(8,128)}, u32[]{:S(2)}) copy-start(f32[8,2048]{1,0:T(8,128)} %mean_ref.1) | copy-start | bytes 196612
  63.3 127.3 %copy-start.7 = (f32[4,2048]{1,0:T(4,128)S(1)}, f32[4,2048]{1,0:T(4,128)}, u32[]{:S(2)}) copy-start(f32[4,2048]{1,0:T(4,128)} %coef_ref.1) | copy-start | bytes 98308
  190.6 2.3 %copy-start = (bf16[3,3,4,256,256]{4,3,2,1,0:T(8,128)(2,1)S(1)}, bf16[3,3,4,256,256]{4,3,2,1,0:T(8,128)(2,1)}, u32[]{:S(2)}) copy-start(bf16[3,3,4,256,256]{4,3,2,1,0:T(8,128)(2,1)} %reduce.1) | copy-start | bytes 14155780
  193.0 3.4 %copy-start.2 = (bf16[8,2048,256]{2,1,0:T(8,128)(2,1)S(1)}, bf16[8,2048,256]{2,1,0:T(8,128)(2,1)}, u32[]{:S(2)}) copy-start(bf16[8,2048,256]{2,1,0:T(8,128)(2,1)} %pert_ref.5) | copy-start | bytes 25165828

commit v2 on v1

v2 whole, which is shorter than its diff:
```python
import functools

import jax
import jax.numpy as jnp
from jax import lax
from jax.experimental import pallas as pl
from jax.experimental.pallas import tpu as pltpu
from jax.sharding import PartitionSpec as P

NS_ITERS = 4
MESH = pl.DeviceIdType.MESH
BIG = 1 << 20
PARTS = ((96, jnp.bfloat16, "xyz"), (96, jnp.bfloat16, "yzx"), (64, jnp.bfloat16, "zxy"), (8, jnp.float32, "zxy"))


def coords():
    a = lax.axis_index("lat")
    b = lax.axis_index("lon")
    return {"y": a // 2, "c": a % 2, "x": b // 4, "z": b % 4}


def device(pos):
    return (pos["y"] * 2 + pos["c"], pos["x"] * 4 + pos["z"])


def shifted(pos, axis, step):
    size = 2 if axis == "c" else 4
    return device({**pos, axis: (pos[axis] + step) % size})


def greet(peers):
    barrier = pltpu.get_barrier_semaphore()
    for peer in peers:
        pl.semaphore_signal(barrier, inc=1, device_id=peer, device_id_type=MESH)
    pl.semaphore_wait(barrier, len(peers))


def lists_kernel(tile_ref, pert_ref, dep_ref, keys_ref, sib_tile_ref, sib_pert_ref, sib_dep_ref,
                 held, send_sem, recv_sem, sib_send, sib_recv):
    pos = coords()
    x, y, z = pos["x"], pos["y"], pos["z"]
    sibling = shifted(pos, "c", 1)
    greet([shifted(pos, axis, step) for axis in "zxy" for step in (1, 2, 3)] + [sibling])
    swaps = []
    for k, (src, dst) in enumerate(((pert_ref, sib_pert_ref), (dep_ref, sib_dep_ref), (tile_ref, sib_tile_ref))):
        swap = pltpu.make_async_remote_copy(
            src_ref=src, dst_ref=dst, send_sem=sib_send.at[k], recv_sem=sib_recv.at[k],
            device_id=sibling, device_id_type=MESH)
        swap.start()
        swaps.append(swap)
    held[y, x, z] = tile_ref[...]
    sent = []
    for phase, axis in enumerate("zxy"):
        view = held.at[y, x, z] if axis == "z" else (held.at[y, x] if axis == "x" else held.at[y])
        copies = []
        for step in (1, 2, 3):
            copy = pltpu.make_async_remote_copy(
                src_ref=view, dst_ref=view, send_sem=send_sem.at[phase, step - 1],
                recv_sem=recv_sem.at[phase, step - 1],
                device_id=shifted(pos, axis, step), device_id_type=MESH)
            copy.start()
            copies.append(copy)
        for copy in copies:
            copy.wait_recv()
        sent += copies
    me = device(pos)
    own = me[0] * 16 + me[1]
    other = sibling[0] * 16 + sibling[1]
    entry = held[...].reshape(64, 8, 128)
    lane = lax.broadcasted_iota(jnp.int32, (64, 8, 128), 2)
    row = lax.broadcasted_iota(jnp.int32, (64, 8, 128), 1)
    owner = entry >> 6
    local_index = entry & 63
    block = jnp.where(owner == own, local_index, local_index + 64)
    value = jnp.where(((owner == own) | (owner == other)) & (row < 4), row * 4096 + lane * 128 + block, BIG)
    out = jnp.full((64, 8, 128), BIG, jnp.int32)
    for k in range(4):
        least = jnp.min(jnp.min(value, axis=2, keepdims=True), axis=1, keepdims=True)
        out = jnp.where(lane == k, least, out)
        value = jnp.where(value > least, value, BIG)
    keys_ref[...] = out
    for copy in sent:
        copy.wait_send()
    for swap in swaps:
        swap.wait()


def gather_lists(tile, pert, dep):
    any_spec = pl.BlockSpec(memory_space=pltpu.HBM)
    vmem = pl.BlockSpec(memory_space=pltpu.VMEM)
    return pl.pallas_call(
        lists_kernel,
        out_shape=(
            jax.ShapeDtypeStruct((64, 8, 128), jnp.int32),
            jax.ShapeDtypeStruct((8, 128), jnp.int32),
            jax.ShapeDtypeStruct(pert.shape, pert.dtype),
            jax.ShapeDtypeStruct(dep.shape, dep.dtype),
        ),
        in_specs=[vmem, any_spec, any_spec],
        out_specs=(vmem, vmem, any_spec, any_spec),
        scratch_shapes=[
            pltpu.VMEM((4, 4, 4, 8, 128), jnp.int32),
            pltpu.SemaphoreType.DMA((3, 3)),
            pltpu.SemaphoreType.DMA((3, 3)),
            pltpu.SemaphoreType.DMA((3,)),
            pltpu.SemaphoreType.DMA((3,)),
        ],
        compiler_params=pltpu.CompilerParams(collective_id=0, has_side_effects=True),
        name="lists",
    )(tile, pert, dep)


def split(value):
    high = value.astype(jnp.bfloat16)
    return high, (value - high.astype(jnp.float32)).astype(jnp.bfloat16)


def product(left, right):
    (lh, ll), (rh, rl) = left, right
    dot = functools.partial(jnp.dot, preferred_element_type=jnp.float32)
    return dot(lh, rh) + (dot(lh, rl) + dot(ll, rh))


def weights_of(g12, packed, extra, members):
    half = members // 2
    row = lax.broadcasted_iota(jnp.int32, (half, half), 0)
    col = lax.broadcasted_iota(jnp.int32, (half, half), 1)
    turned = packed.T
    g11 = jnp.where(col > row, packed, turned)
    g22 = jnp.where(col < row, packed, turned)
    g11 = jnp.where(col == row, extra[0:1], g11)
    g22 = jnp.where(col == row, extra[1:2], g22)
    gram = jnp.concatenate(
        [jnp.concatenate([g11, g12], axis=1), jnp.concatenate([g12.T, g22], axis=1)], axis=0)
    wide_row = lax.broadcasted_iota(jnp.int32, (members, members), 0)
    wide_col = lax.broadcasted_iota(jnp.int32, (members, members), 1)
    identity = jnp.where(wide_row == wide_col, 1.0, 0.0).astype(jnp.float32)
    system = (members - 1.0) * identity + gram
    total = jnp.sum(jnp.sum(system * system, axis=0, keepdims=True), axis=1, keepdims=True)
    scale = jnp.sqrt(total)
    approx = system / scale
    factor = 1.5 * identity - 0.5 * approx
    root = factor
    approx = product(split(approx), split(factor))
    for sweep in range(1, NS_ITERS):
        root_parts = split(root)
        factor = 1.5 * identity - 0.5 * product(root_parts, split(approx))
        factor_parts = split(factor)
        if sweep < NS_ITERS - 1:
            approx = product(split(approx), factor_parts)
        root = product(factor_parts, root_parts)
    innov = jnp.concatenate([extra[2:3], extra[3:4]], axis=1)
    innov = jnp.broadcast_to(innov, (8, members))
    root_parts = split(root)
    inner = product(split(innov), root_parts)
    mean = product(split(inner), root_parts) / scale
    mean_cols = jnp.concatenate(
        [jnp.broadcast_to(mean[:1, :half], (half, half)).T, jnp.broadcast_to(mean[:1, half:], (half, half)).T], axis=0)
    mean_full = jnp.concatenate([mean_cols, mean_cols], axis=1)
    return (jnp.sqrt((members - 1.0) / scale) * root + mean_full).astype(jnp.bfloat16)


def fill_server(place, keys_ref, valid_ref, blocks, deps, grams):
    px, py, pz = place
    base = ((py * 4 + px) * 4 + pz) * 4
    rows = lax.broadcasted_iota(jnp.int32, (128, 256), 0)
    row8 = lax.broadcasted_iota(jnp.int32, (8, 128), 0)
    tri_row = lax.broadcasted_iota(jnp.int32, (128, 128), 0)
    tri_col = lax.broadcasted_iota(jnp.int32, (128, 128), 1)
    held, turned, doms, departs = [], [], [], []
    for j in range(4):
        key = keys_ref[base + j]
        block = key & 127
        dom = key >> 12
        count = jnp.where(key < BIG, valid_ref[block], 0)
        values = jnp.where(rows < count, blocks[block], jnp.zeros((), jnp.bfloat16))
        held.append(values)
        turned.append(values.T)
        doms.append(dom)
        depart = jnp.broadcast_to(deps[pl.ds(block, 1), :], (8, 128))
        departs.append(jnp.where(row8 == dom, depart, 0.0).astype(jnp.bfloat16))
    stacked = jnp.concatenate(held, axis=0)
    inn = jnp.dot(jnp.concatenate(departs, axis=1), stacked, preferred_element_type=jnp.float32)
    for d in range(4):
        left = jnp.concatenate(
            [jnp.where(doms[j] == d, turned[j], jnp.zeros((), jnp.bfloat16)) for j in range(4)], axis=1)
        gram = jnp.dot(left, stacked, preferred_element_type=jnp.float32)
        g11, g12, g22 = gram[:128, :128], gram[:128, 128:], gram[128:, 128:]
        packed = jnp.where(tri_col >= tri_row, g11, g22).astype(jnp.bfloat16)
        g12 = g12.astype(jnp.bfloat16)
        d1 = jnp.sum(jnp.where(tri_col == tri_row, g11, 0.0), axis=0, keepdims=True)
        d2 = jnp.sum(jnp.where(tri_col == tri_row, g22, 0.0), axis=0, keepdims=True)
        grams[0][px, py, pz, pl.ds(d * 96, 96)] = g12[:96]
        grams[1][py, pz, px, pl.ds(d * 96, 32)] = g12[96:]
        grams[1][py, pz, px, pl.ds(d * 96 + 32, 64)] = packed[:64]
        grams[2][pz, px, py, pl.ds(d * 64, 64)] = packed[64:]
        grams[3][pz, px, py, pl.ds(d * 8, 8)] = jnp.concatenate(
            [d1, d2, inn[d:d + 1, :128], inn[d:d + 1, 128:], jnp.zeros((4, 128), jnp.float32)], axis=0)


def reduce_kernel(keys_ref, valid_ref, pert_ref, sib_ref, dep_ref, sib_dep_ref, near_ref, *scratch):
    n = len(PARTS)
    scratch = list(scratch)

    def take(count):
        taken, scratch[:count] = scratch[:count], []
        return taken
    blocks, deps = take(2)
    grams = take(n)
    bufs = [[take(6) for _ in range(n)] for _ in range(3)]
    fins = take(n)
    own, send_sem, recv_sem, load_sem, halo_send, halo_recv, own_sem = scratch

    pos = coords()
    a, b = lax.axis_index("lat"), lax.axis_index("lon")
    lat_up, lat_down = ((a + 1) % 8, b), ((a + 7) % 8, b)
    lon_up, lon_down = (a, (b + 1) % 16), (a, (b + 15) % 16)
    loads = [
        pltpu.make_async_copy(pert_ref, blocks.at[pl.ds(0, 64)], load_sem.at[0]),
        pltpu.make_async_copy(sib_ref, blocks.at[pl.ds(64, 64)], load_sem.at[1]),
    ]
    for load in loads:
        load.start()
    greet([shifted(pos, axis, step) for axis in "xyz" for step in (1, 3)] + [lat_up, lat_down, lon_up, lon_down])
    deps[pl.ds(0, 64)] = dep_ref[...].astype(jnp.float32)
    deps[pl.ds(64, 64)] = sib_dep_ref[...].astype(jnp.float32)
    for load in loads:
        load.wait()

    sends = []
    flights = [[[None] * 6 for _ in range(n)] for _ in range(3)]

    def prefix(i, phase):
        return tuple(pos[axis] for axis in PARTS[i][2][:phase])

    def half(i, phase, target, upper):
        count = (2, 2, 2 * PARTS[i][0])[phase]
        return prefix(i, phase) + (target, pl.ds(count * upper, count))

    def start(i, phase, k, source, to_right):
        copy = pltpu.make_async_remote_copy(
            src_ref=source, dst_ref=bufs[phase][i][k],
            send_sem=send_sem.at[phase, i, k], recv_sem=recv_sem.at[phase, i, k],
            device_id=shifted(pos, PARTS[i][2][phase], 1 if to_right else 3), device_id_type=MESH)
        copy.start()
        sends.append(copy)
        flights[phase][i][k] = copy

    def coord(i, phase):
        return pos[PARTS[i][2][phase]]

    def send_far(i, phase):
        target = (coord(i, phase) + 2) % 4
        start(i, phase, 0, grams[i].at[half(i, phase, target, 0)], True)
        start(i, phase, 1, grams[i].at[half(i, phase, target, 1)], False)

    def send_right(i, phase):
        start(i, phase, 2, grams[i].at[half(i, phase, (coord(i, phase) + 1) % 4, 1)], True)

    def send_left(i, phase):
        start(i, phase, 3, grams[i].at[half(i, phase, (coord(i, phase) + 3) % 4, 0)], False)

    def each(i, phase, body):
        if phase == 0:
            def step(j, carry):
                body((j // 4, j % 4))
                return carry
            lax.fori_loop(0, 8, step, 0)
        elif phase == 1:
            def step(j, carry):
                body((j,))
                return carry
            lax.fori_loop(0, 2, step, 0)
        else:
            body(())

    def local_index(i, phase, target, upper, lead):
        if phase == 2:
            return half(i, phase, target, upper)
        return prefix(i, phase) + (target, 2 * upper + lead[0]) + lead[1:]

    def forward(i, phase):
        m = coord(i, phase)
        for k, (target, upper) in enumerate((((m + 1) % 4, 0), ((m + 3) % 4, 1))):
            flights[phase][i][k].wait_recv()
            got = bufs[phase][i][k]

            def body(lead, got=got, target=target, upper=upper):
                mine = grams[i][local_index(i, phase, target, upper, lead)]
                at = lead if lead else (slice(None),)
                got[at] = (got[at].astype(jnp.float32) + mine.astype(jnp.float32)).astype(got.dtype)
            each(i, phase, body)
            start(i, phase, 4 + k, got, k == 0)

    def finish(i, phase):
        m = coord(i, phase)
        for k in (2, 3, 4, 5):
            flights[phase][i][k].wait_recv()
        for upper, pair in enumerate(((4, 3), (2, 5))):
            f, g = (bufs[phase][i][k] for k in pair)

            def body(lead, f=f, g=g, upper=upper):
                index = local_index(i, phase, m, upper, lead)
                at = lead if lead else (slice(None),)
                total = grams[i][index].astype(jnp.float32) + f[at].astype(jnp.float32) + g[at].astype(jnp.float32)
                if phase < 2:
                    grams[i][index] = total.astype(grams[i].dtype)
                else:
                    fins[i][pl.ds(2 * PARTS[i][0] * upper, 2 * PARTS[i][0])] = total
            each(i, phase, body)

    def fill(count, place):
        def step(j, carry):
            off = place(j)
            fill_server(tuple((pos[axis] + o) % 4 for axis, o in zip("xyz", off)),
                        keys_ref, valid_ref, blocks, deps, grams)
            return carry
        lax.fori_loop(0, count, step, 0)

    fill(16, lambda j: (2, j // 4, j % 4))
    send_far(0, 0)
    fill(12, lambda j: (3 + j // 4, 2, j % 4))
    send_far(1, 0)
    fill(9, lambda j: (3 + j // 3, 3 + j % 3, 2))
    send_far(2, 0)
    send_far(3, 0)
    fill(9, lambda j: (1, 3 + j // 3, 3 + j % 3))
    send_right(0, 0)
    fill(9, lambda j: (3, 3 + j // 3, 3 + j % 3))
    send_left(0, 0)
    fill(9, lambda j: (0, 3 + j // 3, 3 + j % 3))
    for i in range(1, n):
        send_right(i, 0)
        send_left(i, 0)
    for phase in range(3):
        if phase > 0:
            for i in range(n):
                send_far(i, phase)
            for i in range(n):
                send_right(i, phase)
                send_left(i, phase)
        for i in range(n):
            forward(i, phase)
        for i in range(n):
            finish(i, phase)

    def solve(d, carry):
        g12 = jnp.concatenate([fins[0][pl.ds(d * 96, 96)], fins[1][pl.ds(d * 96, 32)]], axis=0)
        packed = jnp.concatenate([fins[1][pl.ds(d * 96 + 32, 64)], fins[2][pl.ds(d * 64, 64)]], axis=0)
        own[d] = weights_of(g12, packed, fins[3][pl.ds(d * 8, 8)], 256)
        return carry
    lax.fori_loop(0, 4, solve, 0)

    keep = pltpu.make_async_copy(own, near_ref.at[1, 1], own_sem)
    keep.start()

    def halo(k, source, dst, target):
        copy = pltpu.make_async_remote_copy(
            src_ref=source, dst_ref=dst, send_sem=halo_send.at[k], recv_sem=halo_recv.at[k],
            device_id=target, device_id_type=MESH)
        copy.start()
        sends.append(copy)
        return copy
    east = halo(0, own, near_ref.at[1, 0], lon_up)
    west = halo(1, own, near_ref.at[1, 2], lon_down)
    arriving = [halo(2, own, near_ref.at[0, 1], lat_up), halo(3, own, near_ref.at[2, 1], lat_down)]
    east.wait_recv()
    arriving += [halo(4, near_ref.at[1, 0], near_ref.at[0, 0], lat_up),
                 halo(5, near_ref.at[1, 0], near_ref.at[2, 0], lat_down)]
    west.wait_recv()
    arriving += [halo(6, near_ref.at[1, 2], near_ref.at[0, 2], lat_up),
                 halo(7, near_ref.at[1, 2], near_ref.at[2, 2], lat_down)]
    for copy in arriving:
        copy.wait_recv()
    for copy in sends:
        copy.wait_send()
    keep.wait()


def near_weights(keys, valid, pert, sib_pert, dep, sib_dep):
    n = len(PARTS)
    hbm = pl.BlockSpec(memory_space=pltpu.HBM)
    smem = pl.BlockSpec(memory_space=pltpu.SMEM)
    full = pl.BlockSpec(memory_space=pltpu.VMEM)

    def vmem(shape, kind):
        return pltpu.VMEM(shape, kind)
    scratch = [vmem((128, 128, 256), jnp.bfloat16), vmem((128, 128), jnp.float32)]
    scratch += [vmem((4, 4, 4, 4 * r, 128), t) for r, t, _ in PARTS]
    for phase in range(3):
        for r, t, _ in PARTS:
            shape = ((2, 4, 4 * r, 128), (2, 4 * r, 128), (2 * r, 128))[phase]
            scratch += [vmem(shape, t)] * 6
    scratch += [vmem((4 * r, 128), jnp.float32) for r, _, _ in PARTS]
    scratch += [
        vmem((4, 256, 256), jnp.bfloat16),
        pltpu.SemaphoreType.DMA((3, n, 6)),
        pltpu.SemaphoreType.DMA((3, n, 6)),
        pltpu.SemaphoreType.DMA((2,)),
        pltpu.SemaphoreType.DMA((8,)),
        pltpu.SemaphoreType.DMA((8,)),
        pltpu.SemaphoreType.DMA(()),
    ]
    return pl.pallas_call(
        reduce_kernel,
        out_shape=jax.ShapeDtypeStruct((3, 3, 4, 256, 256), jnp.bfloat16),
        in_specs=[smem, smem, hbm, hbm, full, full],
        out_specs=hbm,
        scratch_shapes=scratch,
        compiler_params=pltpu.CompilerParams(
            collective_id=1, has_side_effects=True, vmem_limit_bytes=58 << 20),
        name="reduce",
    )(keys, valid, pert, sib_pert, dep, sib_dep)


STEP_TILES = 4


def interp_kernel(pos_ref, pert_ref, mean_ref, coef_ref, near_ref, out_ref):
    step = pl.program_id(0)
    mean_cols = mean_ref[...].T
    coef = coef_ref[...]
    coef_cols = jnp.concatenate([coef, coef], axis=0).T
    for tile in range(STEP_TILES):
        span = pl.ds(tile * 32, 32)
        held = pert_ref[:, span, :].reshape(256, 256)
        total = None
        for corner in range(4):
            where = pos_ref[(step * STEP_TILES + tile) * 4 + corner]
            prod = jnp.dot(held, near_ref[where], preferred_element_type=jnp.float32)
            factor = coef_cols[tile * 32:tile * 32 + 32, corner:corner + 1]
            term = prod.reshape(8, 32, 256) * factor[None]
            total = term if total is None else total + term
        for level in range(8):
            base = mean_cols[tile * 32:tile * 32 + 32, level:level + 1]
            out_ref[level, span, :] = (total[level] + base).astype(jnp.bfloat16)


def interpolate(position, pert, mean, coef, near):
    cols = STEP_TILES * 32
    steps = pert.shape[1] // cols
    return pl.pallas_call(
        interp_kernel,
        out_shape=jax.ShapeDtypeStruct(pert.shape, jnp.bfloat16),
        grid_spec=pltpu.PrefetchScalarGridSpec(
            num_scalar_prefetch=1,
            grid=(steps,),
            in_specs=[
                pl.BlockSpec((8, cols, 256), lambda i, *_: (0, i, 0)),
                pl.BlockSpec((8, cols), lambda i, *_: (0, i)),
                pl.BlockSpec((4, cols), lambda i, *_: (0, i)),
                pl.BlockSpec((36, 256, 256), lambda i, *_: (0, 0, 0), pipeline_mode=pl.Buffered(1)),
            ],
            out_specs=pl.BlockSpec((8, cols, 256), lambda i, *_: (0, i, 0)),
        ),
        compiler_params=pltpu.CompilerParams(
            dimension_semantics=("arbitrary",), vmem_limit_bytes=58 << 20),
        name="interp",
    )(position, pert, mean, coef, near)


def local(
    obs_pert, obs_dep, valid_rows, local_lists, state_mean, state_pert, interp_lists, interp_coef
):
    n_lon = lax.axis_size("lon")
    domains_here = local_lists.shape[0]
    tile = jnp.concatenate([
        jnp.pad(local_lists, ((0, 0), (0, 128 - local_lists.shape[1])), constant_values=-1),
        jnp.pad(valid_rows[None, :], ((0, 3), (0, 64))),
    ], axis=0)
    keys, sib_tile, sib_pert, sib_dep = gather_lists(tile, obs_pert, obs_dep)
    keys = keys[:, 0, :4].reshape(-1)
    valid = jnp.concatenate([valid_rows, sib_tile[4, :64]])
    near = near_weights(keys, valid, obs_pert, sib_pert, obs_dep, sib_dep)
    owner = interp_lists // domains_here
    within = interp_lists % domains_here
    lat_step = owner // n_lon - lax.axis_index("lat")
    lon_step = (owner % n_lon - lax.axis_index("lon") + 1) % n_lon - 1
    position = ((lat_step + 1) * 3 + lon_step + 1) * domains_here + within
    return interpolate(position.reshape(-1), state_pert, state_mean, interp_coef, near.reshape(36, 256, 256))


def solution(mesh):
    in_specs = (
        P(("lat", "lon"), None, None),
        P(("lat", "lon"), None),
        P(("lat", "lon")),
        P(("lat", "lon"), None),
        P(None, ("lat", "lon")),
        P(None, ("lat", "lon"), None),
        P(("lat", "lon"), None),
        P(None, ("lat", "lon")),
    )
    out_specs = P(None, ("lat", "lon"), None)
    return jax.shard_map(local, mesh=mesh, in_specs=in_specs, out_specs=out_specs, check_vma=False)
```

time: 211 us -> 181 us (0.86)
  Pallas kernels: 193 us -> 174 us
  local copies, waits for them, and re-layouts: 15.6 us -> 3.14 us
    pallas_call x1 -> x0, Pallas kernels: 33 us -> none  [partial_grams(): pl.pallas_call(gram_kernel, out_shape=tuple((jax.ShapeDtypeStruct((4, 4,...]
    unnamed x20 -> x0, local copies, waits for them, and re-layouts: 13.6 us -> none
    pallas_call x1, Pallas kernels: 127 us -> 135 us  [near_weights(): pl.pallas_call(reduce_kernel, out_shape=jax.ShapeDtypeStruct((3, 3, 4, 25...]
    pallas_call x1, Pallas kernels: 14.3 us -> 20.1 us  [interpolate(): pl.pallas_call(interp_kernel, out_shape=jax.ShapeDtypeStruct(pert.shape,...]
where the time goes in v2:
time: 181 us; the launch traced here: 180 us
  Pallas kernels  174 us (96%)
  other arithmetic  3.25 us (2%)
  local copies, waits for them, and re-layouts  3.14 us (2%)
    pallas_call x1, Pallas kernels, near_weights(): pl.pallas_call(reduce_kernel, out_shape=jax.ShapeDtypeStruct((3, 3, 4, 25...  135 us
    pallas_call x1, Pallas kernels, interpolate(): pl.pallas_call(interp_kernel, out_shape=jax.ShapeDtypeStruct(pert.shape,...  20.1 us
    pallas_call x1, Pallas kernels, gather_lists(): pl.pallas_call(lists_kernel, out_shape=(jax.ShapeDtypeStruct((64, 8, 128)...  18.7 us

profile of v2, /device:TPU:1, one launch (start us, length us, event | category | flops | bytes accessed | tf_op | source)
XLA Modules:
  0.0 180.5 jit_solution(8571991246133456372)
XLA Ops:
  0.0 0.7 fusion.9
  0.7 1.3 pad_add_fusion.tile_ref
  2.0 0.1 copy.9
  2.1 0.7 reshape.6.pos_ref
  2.8 18.7 %lists.1 = (s32[64,8,128]{2,1,0:T(8,128)}, s32[8,128]{1,0:T(8,128)}, bf16[64,128,256]{2,1,0:T(8,128)(2,1)}, bf16[64,128]{1,0:T(8,128)(2,1)}) custom-call(s32[8,128]{1,0:T(8,128)} %pad_add_fusion.tile_ref, bf16[64,128,256]{2,1,0:T(8,128)(2,1)} %pert_ref.4, bf16[64,128]{1,0:T(8,128)(2,1)} %dep_ref.3), custom_call_target="tpu_custom_call" | custom-call | tf_op jit(solution)/shard_map/lists/pallas_call | solution.py:91
  21.5 1.0 slice_reduce_fusion
  22.5 0.7 reshape_squeeze.3.keys_ref
  23.2 0.7 slice_bitcast_fusion
  23.8 1.2 pad_add_fusion.1.valid_ref
  25.1 135.3 %reduce.5 = bf16[3,3,4,256,256]{4,3,2,1,0:T(8,128)(2,1)} custom-call(s32[256]{0:T(256)} %reshape_squeeze.3.keys_ref, s32[128]{0:T(128)} %pad_add_fusion.1.valid_ref, bf16[64,128,256]{2,1,0:T(8,128)(2,1)} %pert_ref.4, bf16[64,128,256]{2,1,0:T(8,128)(2,1)} %get-tuple-element.11.sib_ref, bf16[64,128]{1,0:T(8,128)(2,1)} %dep_ref.3, ...), custom_call_target="tpu_custom_call" | custom-call | tf_op jit(solution)/shard_map/reduce/pallas_call | solution.py:404
  160.4 20.1 %interp.1 = bf16[8,2048,256]{2,1,0:T(8,128)(2,1)} custom-call(s32[256]{0:T(256)} %reshape.6.pos_ref, bf16[8,2048,256]{2,1,0:T(8,128)(2,1)} %pert_ref.5, f32[8,2048]{1,0:T(8,128)} %mean_ref.1, f32[4,2048]{1,0:T(4,128)} %coef_ref.1, bf16[36,256,256]{2,1,0:T(8,128)(2,1)} %bitcast.4), custom_call_target="tpu_custom_call" | custom-call | tf_op jit(solution)/shard_map/interp/pallas_call | solution.py:442

commit v3 on v2

--- a/solution.py
+++ b/solution.py
@@ -121,43 +121,51 @@
     return dot(lh, rh) + (dot(lh, rl) + dot(ll, rh))
 
 
-def weights_of(g12, packed, extra, members):
+def packed_weights(domains, members):
     half = members // 2
     row = lax.broadcasted_iota(jnp.int32, (half, half), 0)
     col = lax.broadcasted_iota(jnp.int32, (half, half), 1)
-    turned = packed.T
-    g11 = jnp.where(col > row, packed, turned)
-    g22 = jnp.where(col < row, packed, turned)
-    g11 = jnp.where(col == row, extra[0:1], g11)
-    g22 = jnp.where(col == row, extra[1:2], g22)
-    gram = jnp.concatenate(
-        [jnp.concatenate([g11, g12], axis=1), jnp.concatenate([g12.T, g22], axis=1)], axis=0)
     wide_row = lax.broadcasted_iota(jnp.int32, (members, members), 0)
     wide_col = lax.broadcasted_iota(jnp.int32, (members, members), 1)
     identity = jnp.where(wide_row == wide_col, 1.0, 0.0).astype(jnp.float32)
-    system = (members - 1.0) * identity + gram
-    total = jnp.sum(jnp.sum(system * system, axis=0, keepdims=True), axis=1, keepdims=True)
-    scale = jnp.sqrt(total)
-    approx = system / scale
-    factor = 1.5 * identity - 0.5 * approx
-    root = factor
-    approx = product(split(approx), split(factor))
+    scales, approxes = [], []
+    for g12, packed, extra in domains:
+        turned = packed.T
+        g11 = jnp.where(col > row, packed, turned)
+        g22 = jnp.where(col < row, packed, turned)
+        g11 = jnp.where(col == row, extra[0:1], g11)
+        g22 = jnp.where(col == row, extra[1:2], g22)
+        gram = jnp.concatenate(
+            [jnp.concatenate([g11, g12], axis=1), jnp.concatenate([g12.T, g22], axis=1)], axis=0)
+        system = (members - 1.0) * identity + gram
+        scale = jnp.sqrt(jnp.sum(jnp.sum(system * system, axis=0, keepdims=True), axis=1, keepdims=True))
+        scales.append(scale)
+        approxes.append(system / scale)
+    roots = [1.5 * identity - 0.5 * approx for approx in approxes]
+    approxes = [product(split(approx), split(root)) for approx, root in zip(approxes, roots)]
     for sweep in range(1, NS_ITERS):
-        root_parts = split(root)
-        factor = 1.5 * identity - 0.5 * product(root_parts, split(approx))
-        factor_parts = split(factor)
+        root_parts = [split(root) for root in roots]
+        factors = [split(1.5 * identity - 0.5 * product(parts, split(approx)))
+                   for parts, approx in zip(root_parts, approxes)]
         if sweep < NS_ITERS - 1:
-            approx = product(split(approx), factor_parts)
-        root = product(factor_parts, root_parts)
-    innov = jnp.concatenate([extra[2:3], extra[3:4]], axis=1)
-    innov = jnp.broadcast_to(innov, (8, members))
-    root_parts = split(root)
-    inner = product(split(innov), root_parts)
-    mean = product(split(inner), root_parts) / scale
-    mean_cols = jnp.concatenate(
-        [jnp.broadcast_to(mean[:1, :half], (half, half)).T, jnp.broadcast_to(mean[:1, half:], (half, half)).T], axis=0)
-    mean_full = jnp.concatenate([mean_cols, mean_cols], axis=1)
-    return (jnp.sqrt((members - 1.0) / scale) * root + mean_full).astype(jnp.bfloat16)
+            approxes = [product(split(approx), factor) for approx, factor in zip(approxes, factors)]
+        roots = [product(factor, parts) for factor, parts in zip(factors, root_parts)]
+    root_parts = [split(root) for root in roots]
+    innovs = [jnp.broadcast_to(jnp.concatenate([extra[2:3], extra[3:4]], axis=1), (8, members)) for _, _, extra in domains]
+    inners = [product(split(innov), parts) for innov, parts in zip(innovs, root_parts)]
+    means = [product(split(inner), parts) / scale for inner, parts, scale in zip(inners, root_parts, scales)]
+    results = []
+    for root, mean, scale in zip(roots, means, scales):
+        root = jnp.sqrt((members - 1.0) / scale) * root
+        t11, t12, t22 = root[:half, :half], root[:half, half:], root[half:, half:]
+        d2 = jnp.sum(jnp.where(col == row, t22, 0.0), axis=0, keepdims=True)
+        high = mean[:1].astype(jnp.bfloat16).astype(jnp.float32)
+        low = mean[:1] - high
+        rest = jnp.concatenate(
+            [d2, high[:, :half], low[:, :half], high[:, half:], low[:, half:], jnp.zeros((11, half), jnp.float32)], axis=0)
+        results.append((t12.astype(jnp.bfloat16), jnp.where(col >= row, t11, t22).astype(jnp.bfloat16),
+                        rest.astype(jnp.bfloat16)))
+    return results
 
 
 def fill_server(place, keys_ref, valid_ref, blocks, deps, grams):
@@ -344,37 +352,47 @@
         for i in range(n):
             finish(i, phase)
 
-    def solve(d, carry):
-        g12 = jnp.concatenate([fins[0][pl.ds(d * 96, 96)], fins[1][pl.ds(d * 96, 32)]], axis=0)
-        packed = jnp.concatenate([fins[1][pl.ds(d * 96 + 32, 64)], fins[2][pl.ds(d * 64, 64)]], axis=0)
-        own[d] = weights_of(g12, packed, fins[3][pl.ds(d * 8, 8)], 256)
-        return carry
-    lax.fori_loop(0, 4, solve, 0)
-
-    keep = pltpu.make_async_copy(own, near_ref.at[1, 1], own_sem)
-    keep.start()
-
-    def halo(k, source, dst, target):
+    def solve(pair):
+        domains = []
+        for d in pair:
+            g12 = jnp.concatenate([fins[0][pl.ds(d * 96, 96)], fins[1][pl.ds(d * 96, 32)]], axis=0)
+            packed = jnp.concatenate([fins[1][pl.ds(d * 96 + 32, 64)], fins[2][pl.ds(d * 64, 64)]], axis=0)
+            domains.append((g12, packed, fins[3][pl.ds(d * 8, 8)]))
+        for d, (t12, triangles, rest) in zip(pair, packed_weights(domains, 256)):
+            own[d, pl.ds(0, 128)] = t12
+            own[d, pl.ds(128, 128)] = triangles
+            own[d, pl.ds(256, 16)] = rest
+
+    def halo(chunk, k, source, to, target):
         copy = pltpu.make_async_remote_copy(
-            src_ref=source, dst_ref=dst, send_sem=halo_send.at[k], recv_sem=halo_recv.at[k],
+            src_ref=source, dst_ref=near_ref.at[to + (pl.ds(2 * chunk, 2),)],
+            send_sem=halo_send.at[chunk, k], recv_sem=halo_recv.at[chunk, k],
             device_id=target, device_id_type=MESH)
         copy.start()
         sends.append(copy)
         return copy
-    east = halo(0, own, near_ref.at[1, 0], lon_up)
-    west = halo(1, own, near_ref.at[1, 2], lon_down)
-    arriving = [halo(2, own, near_ref.at[0, 1], lat_up), halo(3, own, near_ref.at[2, 1], lat_down)]
-    east.wait_recv()
-    arriving += [halo(4, near_ref.at[1, 0], near_ref.at[0, 0], lat_up),
-                 halo(5, near_ref.at[1, 0], near_ref.at[2, 0], lat_down)]
-    west.wait_recv()
-    arriving += [halo(6, near_ref.at[1, 2], near_ref.at[0, 2], lat_up),
-                 halo(7, near_ref.at[1, 2], near_ref.at[2, 2], lat_down)]
+
+    keeps, sides, arriving = [], [], []
+    for chunk in range(2):
+        solve((2 * chunk, 2 * chunk + 1))
+        mine = own.at[pl.ds(2 * chunk, 2)]
+        sides.append((halo(chunk, 0, mine, (1, 0), lon_up), halo(chunk, 1, mine, (1, 2), lon_down)))
+        arriving += [halo(chunk, 2, mine, (0, 1), lat_up), halo(chunk, 3, mine, (2, 1), lat_down)]
+        keep = pltpu.make_async_copy(mine, near_ref.at[1, 1, pl.ds(2 * chunk, 2)], own_sem.at[chunk])
+        keep.start()
+        keeps.append(keep)
+    for chunk in range(2):
+        for side, column in enumerate((0, 2)):
+            sides[chunk][side].wait_recv()
+            held = near_ref.at[1, column, pl.ds(2 * chunk, 2)]
+            arriving += [halo(chunk, 4 + 2 * side, held, (0, column), lat_up),
+                         halo(chunk, 5 + 2 * side, held, (2, column), lat_down)]
     for copy in arriving:
         copy.wait_recv()
     for copy in sends:
         copy.wait_send()
-    keep.wait()
+    for keep in keeps:
+        keep.wait()
 
 
 def near_weights(keys, valid, pert, sib_pert, dep, sib_dep):
@@ -393,17 +411,17 @@
             scratch += [vmem(shape, t)] * 6
     scratch += [vmem((4 * r, 128), jnp.float32) for r, _, _ in PARTS]
     scratch += [
-        vmem((4, 256, 256), jnp.bfloat16),
+        vmem((4, 272, 128), jnp.bfloat16),
         pltpu.SemaphoreType.DMA((3, n, 6)),
         pltpu.SemaphoreType.DMA((3, n, 6)),
         pltpu.SemaphoreType.DMA((2,)),
-        pltpu.SemaphoreType.DMA((8,)),
-        pltpu.SemaphoreType.DMA((8,)),
-        pltpu.SemaphoreType.DMA(()),
+        pltpu.SemaphoreType.DMA((2, 8)),
+        pltpu.SemaphoreType.DMA((2, 8)),
+        pltpu.SemaphoreType.DMA((2,)),
     ]
     return pl.pallas_call(
         reduce_kernel,
-        out_shape=jax.ShapeDtypeStruct((3, 3, 4, 256, 256), jnp.bfloat16),
+        out_shape=jax.ShapeDtypeStruct((3, 3, 4, 272, 128), jnp.bfloat16),
         in_specs=[smem, smem, hbm, hbm, full, full],
         out_specs=hbm,
         scratch_shapes=scratch,
@@ -416,21 +434,46 @@
 STEP_TILES = 4
 
 
-def interp_kernel(pos_ref, pert_ref, mean_ref, coef_ref, near_ref, out_ref):
+def interp_kernel(pos_ref, pert_ref, mean_ref, coef_ref, near_ref, out_ref, tiles):
     step = pl.program_id(0)
+
+    @pl.when(step == 0)
+    def _():
+        row = lax.broadcasted_iota(jnp.int32, (128, 128), 0)
+        col = lax.broadcasted_iota(jnp.int32, (128, 128), 1)
+
+        def unpack(k, carry):
+            t12 = near_ref[k, pl.ds(0, 128)]
+            packed = near_ref[k, pl.ds(128, 128)]
+            rest = near_ref[k, pl.ds(256, 16)].astype(jnp.float32)
+            columns = rest.T
+            first = columns[:, 1:2] + columns[:, 2:3]
+            second = columns[:, 3:4] + columns[:, 4:5]
+            packed = packed.astype(jnp.float32)
+            turned = packed.T
+            t11 = jnp.where(col >= row, packed, turned)
+            t22 = jnp.where(col < row, packed, jnp.where(col == row, rest[0:1], turned))
+            wide = t12.astype(jnp.float32)
+            tiles[k, pl.ds(0, 128), pl.ds(0, 128)] = (t11 + first).astype(jnp.bfloat16)
+            tiles[k, pl.ds(0, 128), pl.ds(128, 128)] = (wide + first).astype(jnp.bfloat16)
+            tiles[k, pl.ds(128, 128), pl.ds(0, 128)] = (wide.T + second).astype(jnp.bfloat16)
+            tiles[k, pl.ds(128, 128), pl.ds(128, 128)] = (t22 + second).astype(jnp.bfloat16)
+            return carry
+        lax.fori_loop(0, 36, unpack, 0)
+
     mean_cols = mean_ref[...].T
     coef = coef_ref[...]
     coef_cols = jnp.concatenate([coef, coef], axis=0).T
     for tile in range(STEP_TILES):
         span = pl.ds(tile * 32, 32)
-        held = pert_ref[:, span, :].reshape(256, 256)
-        total = None
+        held = pert_ref[:, span, :].astype(jnp.float32)
+        lefts, rights = [], []
         for corner in range(4):
-            where = pos_ref[(step * STEP_TILES + tile) * 4 + corner]
-            prod = jnp.dot(held, near_ref[where], preferred_element_type=jnp.float32)
             factor = coef_cols[tile * 32:tile * 32 + 32, corner:corner + 1]
-            term = prod.reshape(8, 32, 256) * factor[None]
-            total = term if total is None else total + term
+            lefts.append((held * factor[None]).astype(jnp.bfloat16).reshape(256, 256))
+            rights.append(tiles[pos_ref[(step * STEP_TILES + tile) * 4 + corner]])
+        total = jnp.dot(jnp.concatenate(lefts, axis=1), jnp.concatenate(rights, axis=0),
+                        preferred_element_type=jnp.float32).reshape(8, 32, 256)
         for level in range(8):
             base = mean_cols[tile * 32:tile * 32 + 32, level:level + 1]
             out_ref[level, span, :] = (total[level] + base).astype(jnp.bfloat16)
@@ -449,9 +492,10 @@
                 pl.BlockSpec((8, cols, 256), lambda i, *_: (0, i, 0)),
                 pl.BlockSpec((8, cols), lambda i, *_: (0, i)),
                 pl.BlockSpec((4, cols), lambda i, *_: (0, i)),
-                pl.BlockSpec((36, 256, 256), lambda i, *_: (0, 0, 0), pipeline_mode=pl.Buffered(1)),
+                pl.BlockSpec((36, 272, 128), lambda i, *_: (0, 0, 0), pipeline_mode=pl.Buffered(1)),
             ],
             out_specs=pl.BlockSpec((8, cols, 256), lambda i, *_: (0, i, 0)),
+            scratch_shapes=[pltpu.VMEM((36, 256, 256), jnp.bfloat16)],
         ),
         compiler_params=pltpu.CompilerParams(
             dimension_semantics=("arbitrary",), vmem_limit_bytes=58 << 20),
@@ -477,7 +521,7 @@
     lat_step = owner // n_lon - lax.axis_index("lat")
     lon_step = (owner % n_lon - lax.axis_index("lon") + 1) % n_lon - 1
     position = ((lat_step + 1) * 3 + lon_step + 1) * domains_here + within
-    return interpolate(position.reshape(-1), state_pert, state_mean, interp_coef, near.reshape(36, 256, 256))
+    return interpolate(position.reshape(-1), state_pert, state_mean, interp_coef, near.reshape(36, 272, 128))
 
 
 def solution(mesh):

time: 181 us -> 176 us (0.972)
  Pallas kernels: 174 us -> 168 us
    pallas_call x1, Pallas kernels: 135 us -> 120 us  [near_weights(): pl.pallas_call(reduce_kernel, out_shape=jax.ShapeDtypeStruct((3, 3, 4, 27...]
    pallas_call x1, Pallas kernels: 20.1 us -> 29.9 us  [interpolate(): pl.pallas_call(interp_kernel, out_shape=jax.ShapeDtypeStruct(pert.shape,...]
where the time goes in v3:
time: 176 us; the launch traced here: 174 us
  Pallas kernels  168 us (95%)
  local copies, waits for them, and re-layouts  3.17 us (2%)
  other arithmetic  2.68 us (2%)
    pallas_call x1, Pallas kernels, near_weights(): pl.pallas_call(reduce_kernel, out_shape=jax.ShapeDtypeStruct((3, 3, 4, 27...  120 us
    pallas_call x1, Pallas kernels, interpolate(): pl.pallas_call(interp_kernel, out_shape=jax.ShapeDtypeStruct(pert.shape,...  29.9 us
    pallas_call x1, Pallas kernels, gather_lists(): pl.pallas_call(lists_kernel, out_shape=(jax.ShapeDtypeStruct((64, 8, 128)...  18.7 us

profile of v3, /device:TPU:1, one launch (start us, length us, event | category | flops | bytes accessed | tf_op | source)
XLA Modules:
  0.0 174.3 jit_solution(15556169718990638879)
XLA Ops:
  0.0 0.0 copy-start
  0.0 0.7 fusion.9
  0.7 1.3 pad_add_fusion.tile_ref
  2.0 0.1 copy.9
  2.1 0.7 reshape.6.pos_ref
  2.8 18.7 %lists.1 = (s32[64,8,128]{2,1,0:T(8,128)}, s32[8,128]{1,0:T(8,128)}, bf16[64,128,256]{2,1,0:T(8,128)(2,1)}, bf16[64,128]{1,0:T(8,128)(2,1)}) custom-call(s32[8,128]{1,0:T(8,128)} %pad_add_fusion.tile_ref, bf16[64,128,256]{2,1,0:T(8,128)(2,1)} %pert_ref.4, bf16[64,128]{1,0:T(8,128)(2,1)} %dep_ref.3), custom_call_target="tpu_custom_call" | custom-call | tf_op jit(solution)/shard_map/lists/pallas_call | solution.py:91
  21.5 1.0 slice_reduce_fusion
  22.5 0.7 reshape_squeeze.3.keys_ref
  23.2 0.7 slice_bitcast_fusion
  23.9 0.0 copy-done
  23.9 0.7 pad_add_fusion.1.valid_ref
  24.5 119.8 %reduce.5 = bf16[3,3,4,272,128]{4,3,2,1,0:T(8,128)(2,1)} custom-call(s32[256]{0:T(256)} %reshape_squeeze.3.keys_ref, s32[128]{0:T(128)} %pad_add_fusion.1.valid_ref, bf16[64,128,256]{2,1,0:T(8,128)(2,1)} %pert_ref.4, bf16[64,128,256]{2,1,0:T(8,128)(2,1)} %get-tuple-element.11.sib_ref, bf16[64,128]{1,0:T(8,128)(2,1)} %dep_ref.3, ...), custom_call_target="tpu_custom_call" | custom-call | tf_op jit(solution)/shard_map/reduce/pallas_call | solution.py:422
  144.4 29.9 %interp.1 = bf16[8,2048,256]{2,1,0:T(8,128)(2,1)} custom-call(s32[256]{0:T(256)} %reshape.6.pos_ref, bf16[8,2048,256]{2,1,0:T(8,128)(2,1)} %pert_ref.5, f32[8,2048]{1,0:T(8,128)} %mean_ref.1, f32[4,2048]{1,0:T(4,128)} %coef_ref.1, bf16[36,272,128]{2,1,0:T(8,128)(2,1)} %bitcast.4), custom_call_target="tpu_custom_call" | custom-call | tf_op jit(solution)/shard_map/interp/pallas_call | solution.py:485
Async XLA Ops:
  0.0 23.9 %copy-start = (s32[64]{0:T(128)S(1)}, s32[64]{0:T(128)}, u32[]{:S(2)}) copy-start(s32[64]{0:T(128)} %param.10) | copy-start | bytes 772

commit v4 on v3

v4 whole, which is shorter than its diff:
```python
import functools

import jax
import jax.numpy as jnp
from jax import lax
from jax.experimental import pallas as pl
from jax.experimental.pallas import tpu as pltpu
from jax.sharding import PartitionSpec as P

NS_ITERS = 4
MESH = pl.DeviceIdType.MESH
BIG = 1 << 20
PARTS = ((400, jnp.bfloat16, "xyz"), (352, jnp.bfloat16, "yzx"), (272, jnp.bfloat16, "zxy"), (16, jnp.float32, "zxy"))
STARTS = (0, 400, 752)


def coords():
    a = lax.axis_index("lat")
    b = lax.axis_index("lon")
    return {"y": a // 2, "c": a % 2, "x": b // 4, "z": b % 4}


def device(pos):
    return (pos["y"] * 2 + pos["c"], pos["x"] * 4 + pos["z"])


def shifted(pos, axis, step):
    size = 2 if axis == "c" else 4
    return device({**pos, axis: (pos[axis] + step) % size})


def greet(peers):
    barrier = pltpu.get_barrier_semaphore()
    for peer in peers:
        pl.semaphore_signal(barrier, inc=1, device_id=peer, device_id_type=MESH)
    pl.semaphore_wait(barrier, len(peers))


def split(value):
    high = value.astype(jnp.bfloat16)
    return high, (value - high.astype(jnp.float32)).astype(jnp.bfloat16)


def product(left, right):
    (lh, ll), (rh, rl) = left, right
    dot = functools.partial(jnp.dot, preferred_element_type=jnp.float32)
    return dot(lh, rh) + (dot(lh, rl) + dot(ll, rh))


def packed_weights(domains, members, between):
    half = members // 2
    row = lax.broadcasted_iota(jnp.int32, (half, half), 0)
    col = lax.broadcasted_iota(jnp.int32, (half, half), 1)
    wide_row = lax.broadcasted_iota(jnp.int32, (members, members), 0)
    wide_col = lax.broadcasted_iota(jnp.int32, (members, members), 1)
    identity = jnp.where(wide_row == wide_col, 1.0, 0.0).astype(jnp.float32)
    scales, approxes = [], []
    for g12, packed, extra in domains:
        turned = packed.T
        g11 = jnp.where(col > row, packed, turned)
        g22 = jnp.where(col < row, packed, turned)
        g11 = jnp.where(col == row, extra[0:1], g11)
        g22 = jnp.where(col == row, extra[1:2], g22)
        gram = jnp.concatenate(
            [jnp.concatenate([g11, g12], axis=1), jnp.concatenate([g12.T, g22], axis=1)], axis=0)
        system = (members - 1.0) * identity + gram
        scale = jnp.sqrt(jnp.sum(jnp.sum(system * system, axis=0, keepdims=True), axis=1, keepdims=True))
        scales.append(scale)
        approxes.append(system / scale)
    roots = [1.5 * identity - 0.5 * approx for approx in approxes]
    approxes = [product(split(approx), split(root)) for approx, root in zip(approxes, roots)]
    for sweep in range(1, NS_ITERS):
        root_parts = [split(root) for root in roots]
        factors = [split(1.5 * identity - 0.5 * product(parts, split(approx)))
                   for parts, approx in zip(root_parts, approxes)]
        if sweep < NS_ITERS - 1:
            approxes = [product(split(approx), factor) for approx, factor in zip(approxes, factors)]
        roots = [product(factor, parts) for factor, parts in zip(factors, root_parts)]
        if sweep == 2:
            between()
    root_parts = [split(root) for root in roots]
    innovs = [jnp.broadcast_to(jnp.concatenate([extra[2:3], extra[3:4]], axis=1), (8, members)) for _, _, extra in domains]
    inners = [product(split(innov), parts) for innov, parts in zip(innovs, root_parts)]
    means = [product(split(inner), parts) / scale for inner, parts, scale in zip(inners, root_parts, scales)]
    results = []
    for root, mean, scale in zip(roots, means, scales):
        root = jnp.sqrt((members - 1.0) / scale) * root
        t11, t12, t22 = root[:half, :half], root[:half, half:], root[half:, half:]
        exact = [jnp.sum(jnp.where(col == row, t, 0.0), axis=0, keepdims=True) for t in (t11, t22)]
        exact += [mean[:1, :half], mean[:1, half:]]
        highs = [value.astype(jnp.bfloat16).astype(jnp.float32) for value in exact]
        lows = [value - high for value, high in zip(exact, highs)]
        rest = jnp.concatenate(highs + lows + [jnp.zeros((8, half), jnp.float32)], axis=0)
        results.append((t12.astype(jnp.bfloat16), jnp.where(col >= row, t11, t22).astype(jnp.bfloat16),
                        rest.astype(jnp.bfloat16)))
    return results


def store_rows(refs, index, first, value):
    count = value.shape[0]
    for i, start in enumerate(STARTS):
        low, high = max(first, start), min(first + count, start + PARTS[i][0])
        if low < high:
            refs[i][index[i] + (pl.ds(low - start, high - low),)] = value[low - first:high - first]


def fill_server(place, keys_ref, valid_ref, blocks, deps, grams):
    px, py, pz = place
    server = (py * 4 + px) * 4 + pz
    index = ((px, py, pz), (py, pz, px), (pz, px, py))
    rows = lax.broadcasted_iota(jnp.int32, (128, 256), 0)
    row8 = lax.broadcasted_iota(jnp.int32, (8, 128), 0)
    tri_row = lax.broadcasted_iota(jnp.int32, (128, 128), 0)
    tri_col = lax.broadcasted_iota(jnp.int32, (128, 128), 1)
    held, turned, doms, departs = [], [], [], []
    for j in range(4):
        key = keys_ref[server, j]
        block = key & 127
        dom = key >> 12
        count = jnp.where(key < BIG, valid_ref[block >> 6, 4, block & 63], 0)
        values = jnp.where(rows < count, blocks[block], jnp.zeros((), jnp.bfloat16))
        held.append(values)
        turned.append(values.T)
        doms.append(dom)
        depart = jnp.broadcast_to(deps[pl.ds(block, 1), :], (8, 128))
        departs.append(jnp.where(row8 == dom, depart, 0.0).astype(jnp.bfloat16))
    stacked = jnp.concatenate(held, axis=0)
    inn = jnp.dot(jnp.concatenate(departs, axis=1), stacked, preferred_element_type=jnp.float32)
    for d in range(4):
        left = jnp.concatenate(
            [jnp.where(doms[j] == d, turned[j], jnp.zeros((), jnp.bfloat16)) for j in range(4)], axis=1)
        gram = jnp.dot(left, stacked, preferred_element_type=jnp.float32)
        g11, g12, g22 = gram[:128, :128], gram[:128, 128:], gram[128:, 128:]
        packed = jnp.where(tri_col >= tri_row, g11, g22).astype(jnp.bfloat16)
        g12 = g12.astype(jnp.bfloat16)
        d1 = jnp.sum(jnp.where(tri_col == tri_row, g11, 0.0), axis=0, keepdims=True)
        d2 = jnp.sum(jnp.where(tri_col == tri_row, g22, 0.0), axis=0, keepdims=True)
        store_rows(grams, index, d * 256, g12)
        store_rows(grams, index, d * 256 + 128, packed)
        grams[3][pz, px, py, pl.ds(d * 4, 4)] = jnp.concatenate(
            [d1, d2, inn[d:d + 1, :128], inn[d:d + 1, 128:]], axis=0)


def listed_keys(held, own, other):
    lane = lax.broadcasted_iota(jnp.int32, (64, 128), 1)
    values = []
    for dom in range(4):
        entry = held[:, dom, :]
        owner, local_index = entry >> 6, entry & 63
        block = jnp.where(owner == own, local_index, local_index + 64)
        values.append(jnp.where((owner == own) | (owner == other), dom * 4096 + lane * 128 + block, BIG))
    out = jnp.full((64, 128), BIG, jnp.int32)
    for k in range(4):
        least = functools.reduce(jnp.minimum, values)
        least = jnp.min(least, axis=1, keepdims=True)
        out = jnp.where(lane == k, least, out)
        values = [jnp.where(value > least, value, BIG) for value in values]
    return out


def full_weights(packed_ref, index, tiles, k):
    row = lax.broadcasted_iota(jnp.int32, (128, 128), 0)
    col = lax.broadcasted_iota(jnp.int32, (128, 128), 1)
    wide = packed_ref[index + (pl.ds(0, 128),)].astype(jnp.float32)
    packed = packed_ref[index + (pl.ds(128, 128),)].astype(jnp.float32)
    rest = packed_ref[index + (pl.ds(256, 16),)].astype(jnp.float32)
    rest = rest[:4] + rest[4:8]
    columns = jnp.concatenate([rest, rest], axis=0).T
    first, second = columns[:, 2:3], columns[:, 3:4]
    turned = packed.T
    t11 = jnp.where(col > row, packed, jnp.where(col == row, rest[0:1], turned))
    t22 = jnp.where(col < row, packed, jnp.where(col == row, rest[1:2], turned))
    left, right = pl.ds(0, 128), pl.ds(128, 128)
    tiles[2 * k, :, left] = (t11 + first).astype(jnp.bfloat16)
    tiles[2 * k, :, right] = (wide + first).astype(jnp.bfloat16)
    tiles[2 * k + 1, :, left] = (wide.T + second).astype(jnp.bfloat16)
    tiles[2 * k + 1, :, right] = (t22 + second).astype(jnp.bfloat16)


def reduce_kernel(tile_ref, pert_ref, dep_ref, out_ref, *scratch):
    n = len(PARTS)
    scratch = list(scratch)

    def take(count):
        taken, scratch[:count] = scratch[:count], []
        return taken
    held, keys_vmem, keys_ref, valid_ref, sib_tile, sib_dep, blocks, deps, near, fin, fin_extra = take(11)
    grams = take(n)
    bufs = [[take(6) for _ in range(n)] for _ in range(2)] + [[take(3) for _ in range(n)]]
    send_sem, recv_sem, load_sem, list_send, list_recv, sib_send, sib_recv, halo_send, halo_recv, out_sem = scratch

    pos = coords()
    x, y, z = pos["x"], pos["y"], pos["z"]
    a, b = lax.axis_index("lat"), lax.axis_index("lon")
    lat_up, lat_down = ((a + 1) % 8, b), ((a + 7) % 8, b)
    lon_up, lon_down = (a, (b + 1) % 16), (a, (b + 15) % 16)
    sibling = shifted(pos, "c", 1)
    load = pltpu.make_async_copy(pert_ref, blocks.at[pl.ds(0, 64)], load_sem.at[0])
    load.start()
    own_valid = pltpu.make_async_copy(tile_ref, valid_ref.at[0], load_sem.at[1])
    own_valid.start()
    me = (y * 4 + x) * 4 + z
    held[me] = tile_ref[...]
    deps[pl.ds(0, 64)] = dep_ref[...].astype(jnp.float32)
    greet([shifted(pos, axis, step) for axis in "zxy" for step in (1, 2, 3)]
          + [sibling, lat_up, lat_down, lon_up, lon_down])

    sends = []

    def swap(k, src, dst):
        copy = pltpu.make_async_remote_copy(
            src_ref=src, dst_ref=dst, send_sem=sib_send.at[k], recv_sem=sib_recv.at[k],
            device_id=sibling, device_id_type=MESH)
        copy.start()
        sends.append(copy)
        return copy
    swaps = [swap(0, tile_ref, sib_tile), swap(1, dep_ref, sib_dep), swap(2, pert_ref, blocks.at[pl.ds(64, 64)])]
    for phase, (axis, first, count) in enumerate((("z", me, 1), ("x", (y * 4 + x) * 4, 4), ("y", y * 16, 16))):
        view = held.at[pl.ds(first, count)]
        copies = []
        for step in (1, 2, 3):
            copy = pltpu.make_async_remote_copy(
                src_ref=view, dst_ref=view, send_sem=list_send.at[phase, step - 1],
                recv_sem=list_recv.at[phase, step - 1],
                device_id=shifted(pos, axis, step), device_id_type=MESH)
            copy.start()
            copies.append(copy)
        for copy in copies:
            copy.wait_recv()
        sends += copies
    keys_vmem[...] = listed_keys(held, a * 16 + b, sibling[0] * 16 + sibling[1])
    keys_copy = pltpu.make_async_copy(keys_vmem, keys_ref, load_sem.at[2])
    keys_copy.start()
    swaps[0].wait_recv()
    sib_valid = pltpu.make_async_copy(sib_tile, valid_ref.at[1], load_sem.at[3])
    sib_valid.start()
    swaps[1].wait_recv()
    deps[pl.ds(64, 64)] = sib_dep[...].astype(jnp.float32)
    for copy in (own_valid, keys_copy, sib_valid, load):
        copy.wait()
    swaps[2].wait_recv()

    flights = [[[None] * 6 for _ in range(n)] for _ in range(2)]

    def prefix(i, phase):
        return tuple(pos[axis] for axis in PARTS[i][2][:phase])

    def half(i, phase, target, upper):
        return prefix(i, phase) + (target, pl.ds(2 * upper, 2))

    def start(i, phase, k, source, to_right):
        copy = pltpu.make_async_remote_copy(
            src_ref=source, dst_ref=bufs[phase][i][k],
            send_sem=send_sem.at[phase, i, k], recv_sem=recv_sem.at[phase, i, k],
            device_id=shifted(pos, PARTS[i][2][phase], 1 if to_right else 3), device_id_type=MESH)
        copy.start()
        sends.append(copy)
        flights[phase][i][k] = copy

    def coord(i, phase):
        return pos[PARTS[i][2][phase]]

    def send_far(i, phase, sides=(0, 1)):
        target = (coord(i, phase) + 2) % 4
        for side in sides:
            start(i, phase, side, grams[i].at[half(i, phase, target, side)], side == 0)

    def send_right(i, phase):
        start(i, phase, 2, grams[i].at[half(i, phase, (coord(i, phase) + 1) % 4, 1)], True)

    def send_left(i, phase):
        start(i, phase, 3, grams[i].at[half(i, phase, (coord(i, phase) + 3) % 4, 0)], False)

    def each(phase, body):
        def step(j, carry):
            body((j // 4, j % 4) if phase == 0 else (j,))
            return carry
        lax.fori_loop(0, 8 if phase == 0 else 2, step, 0)

    def local_index(i, phase, target, upper, lead):
        return prefix(i, phase) + (target, 2 * upper + lead[0]) + lead[1:]

    def forward(i, phase):
        m = coord(i, phase)
        for k, (target, upper) in enumerate((((m + 1) % 4, 0), ((m + 3) % 4, 1))):
            flights[phase][i][k].wait_recv()
            got = bufs[phase][i][k]

            def body(lead, got=got, target=target, upper=upper):
                mine = grams[i][local_index(i, phase, target, upper, lead)]
                got[lead] = (got[lead].astype(jnp.float32) + mine.astype(jnp.float32)).astype(got.dtype)
            each(phase, body)
            start(i, phase, 4 + k, got, k == 0)

    def finish(i, phase):
        m = coord(i, phase)
        for k in (2, 3, 4, 5):
            flights[phase][i][k].wait_recv()
        for upper, pair in enumerate(((4, 3), (2, 5))):
            f, g = (bufs[phase][i][k] for k in pair)

            def body(lead, f=f, g=g, upper=upper):
                index = local_index(i, phase, m, upper, lead)
                total = grams[i][index].astype(jnp.float32) + f[lead].astype(jnp.float32) + g[lead].astype(jnp.float32)
                grams[i][index] = total.astype(grams[i].dtype)
            each(phase, body)

    def send_last(i):
        copies = []
        for step in (1, 2, 3):
            copy = pltpu.make_async_remote_copy(
                src_ref=grams[i].at[prefix(i, 2) + ((coord(i, 2) + step) % 4,)], dst_ref=bufs[2][i][step - 1],
                send_sem=send_sem.at[2, i, step - 1], recv_sem=recv_sem.at[2, i, step - 1],
                device_id=shifted(pos, PARTS[i][2][2], step), device_id_type=MESH)
            copy.start()
            copies.append(copy)
        sends.extend(copies)
        return copies

    def finish_last(i, copies):
        for copy in copies:
            copy.wait_recv()
        total = grams[i][prefix(i, 2) + (coord(i, 2),)].astype(jnp.float32)
        for got in bufs[2][i]:
            total = total + got[...].astype(jnp.float32)
        if i < 3:
            fin[pl.ds(STARTS[i], PARTS[i][0])] = total
        else:
            fin_extra[...] = total

    def fill(count, place):
        def step(j, carry):
            fill_server(tuple(at % 4 for at in place(j)), keys_ref, valid_ref, blocks, deps, grams)
            return carry
        lax.fori_loop(0, count, step, 0)

    fill(8, lambda j: (x + 2, j // 4, z + j))
    send_far(0, 0, (0,))
    fill(8, lambda j: (x + 2, 2 + j // 4, z + j))
    send_far(0, 0, (1,))
    fill(6, lambda j: (x + 3 + j % 3, y + 2, j // 3))
    send_far(1, 0, (0,))
    fill(6, lambda j: (x + 3 + j % 3, y + 2, 2 + j // 3))
    send_far(1, 0, (1,))
    fill(9, lambda j: (x + 3 + j // 3, y + 3 + j % 3, z + 2))
    send_far(2, 0)
    send_far(3, 0)
    fill(9, lambda j: (x + 1, y + 3 + j // 3, z + 3 + j % 3))
    send_right(0, 0)
    fill(9, lambda j: (x + 3, y + 3 + j // 3, z + 3 + j % 3))
    send_left(0, 0)
    fill(3, lambda j: (x, y + 1, z + 3 + j))
    send_right(1, 0)
    fill(3, lambda j: (x, y + 3, z + 3 + j))
    send_left(1, 0)
    fill(3, lambda j: (x, y, z + 3 + j))
    for i in (2, 3):
        send_right(i, 0)
        send_left(i, 0)
    for i in range(n):
        forward(i, 0)
    for i in range(n):
        finish(i, 0)
        send_far(i, 1)
        send_right(i, 1)
        send_left(i, 1)
    for i in range(n):
        forward(i, 1)
    last = []
    for i in range(n):
        finish(i, 1)
        last.append(send_last(i))
    for i in range(n):
        finish_last(i, last[i])

    def solve(pair, between):
        domains = [(fin[pl.ds(d * 256, 128)], fin[pl.ds(d * 256 + 128, 128)], fin_extra[pl.ds(d * 4, 4)]) for d in pair]
        for d, (t12, triangles, rest) in zip(pair, packed_weights(domains, 256, between)):
            near[1, 1, d, pl.ds(0, 128)] = t12
            near[1, 1, d, pl.ds(128, 128)] = triangles
            near[1, 1, d, pl.ds(256, 16)] = rest

    halos = {}

    def halo(chunk, k, origin, to, target):
        span = pl.ds(2 * chunk, 2)
        copy = pltpu.make_async_remote_copy(
            src_ref=near.at[origin + (span,)], dst_ref=near.at[to + (span,)],
            send_sem=halo_send.at[chunk, k], recv_sem=halo_recv.at[chunk, k],
            device_id=target, device_id_type=MESH)
        copy.start()
        sends.append(copy)
        halos[chunk, to] = copy

    outs = []

    def unpack(chunk, at):
        first = (at[0] * 3 + at[1]) * 4 + 2 * chunk
        for k in range(2):
            full_weights(near, at + (2 * chunk + k,), blocks, first + k)
        copy = pltpu.make_async_copy(
            blocks.at[pl.ds(2 * first, 4)], out_ref.at[pl.ds(2 * first, 4)], out_sem.at[len(outs)])
        copy.start()
        outs.append(copy)

    def own_halo(chunk):
        halo(chunk, 0, (1, 1), (1, 0), lon_up)
        halo(chunk, 1, (1, 1), (1, 2), lon_down)
        halo(chunk, 2, (1, 1), (0, 1), lat_up)
        halo(chunk, 3, (1, 1), (2, 1), lat_down)

    def corner_halo(chunk):
        for column, k in ((0, 4), (2, 6)):
            halos[chunk, (1, column)].wait_recv()
            halo(chunk, k, (1, column), (0, column), lat_up)
            halo(chunk, k + 1, (1, column), (2, column), lat_down)

    solve((0, 1), lambda: None)
    own_halo(0)
    solve((2, 3), lambda: corner_halo(0))
    own_halo(1)
    for chunk in range(2):
        unpack(chunk, (1, 1))
    for column in (0, 2):
        unpack(0, (1, column))
    corner_halo(1)
    for column in (0, 2):
        unpack(1, (1, column))
    for chunk in range(2):
        for column in (1, 0, 2):
            for line in (0, 2):
                halos[chunk, (line, column)].wait_recv()
                unpack(chunk, (line, column))
    for copy in sends:
        copy.wait_send()
    for copy in outs:
        copy.wait()


def near_weights(tile, pert, dep):
    n = len(PARTS)
    hbm = pl.BlockSpec(memory_space=pltpu.HBM)
    full = pl.BlockSpec(memory_space=pltpu.VMEM)

    def vmem(shape, kind):
        return pltpu.VMEM(shape, kind)
    scratch = [
        vmem((64, 8, 128), jnp.int32),
        vmem((64, 128), jnp.int32),
        pltpu.SMEM((64, 128), jnp.int32),
        pltpu.SMEM((2, 8, 128), jnp.int32),
        vmem((8, 128), jnp.int32),
        vmem((64, 128), jnp.bfloat16),
        vmem((128, 128, 256), jnp.bfloat16),
        vmem((128, 128), jnp.float32),
        vmem((3, 3, 4, 272, 128), jnp.bfloat16),
        vmem((1024, 128), jnp.float32),
        vmem((16, 128), jnp.float32),
    ]
    scratch += [vmem((4, 4, 4, r, 128), t) for r, t, _ in PARTS]
    for shape in ((2, 4), (2,)):
        for r, t, _ in PARTS:
            scratch += [vmem(shape + (r, 128), t)] * 6
    for r, t, _ in PARTS:
        scratch += [vmem((r, 128), t)] * 3
    scratch += [pltpu.SemaphoreType.DMA(shape) for shape in (
        (3, n, 6), (3, n, 6), (4,), (3, 3), (3, 3), (3,), (3,), (2, 8), (2, 8), (18,))]
    return pl.pallas_call(
        reduce_kernel,
        out_shape=jax.ShapeDtypeStruct((72, 128, 256), jnp.bfloat16),
        in_specs=[full, hbm, full],
        out_specs=hbm,
        scratch_shapes=scratch,
        compiler_params=pltpu.CompilerParams(
            collective_id=1, has_side_effects=True, vmem_limit_bytes=58 << 20),
        name="reduce",
    )(tile, pert, dep)


STEP_TILES = 4


def interp_kernel(pos_ref, pert_ref, mean_ref, coef_ref, near_ref, out_ref):
    step = pl.program_id(0)
    mean_cols = mean_ref[...].T
    coef = coef_ref[...]
    coef_cols = jnp.concatenate([coef, coef], axis=0).T
    for tile in range(STEP_TILES):
        span = pl.ds(tile * 32, 32)
        held = pert_ref[:, span, :].reshape(256, 256)
        total = None
        for pair in ((0, 1), (2, 3)):
            near = [near_ref[pos_ref[(step * STEP_TILES + tile) * 4 + corner]] for corner in pair]
            both = jnp.dot(held, jnp.concatenate(near, axis=1), preferred_element_type=jnp.float32)
            for k, corner in enumerate(pair):
                factor = coef_cols[tile * 32:tile * 32 + 32, corner:corner + 1]
                term = both[:, 256 * k:256 * k + 256].reshape(8, 32, 256) * factor[None]
                total = term if total is None else total + term
        for level in range(8):
            base = mean_cols[tile * 32:tile * 32 + 32, level:level + 1]
            out_ref[level, span, :] = (total[level] + base).astype(jnp.bfloat16)


def interpolate(position, pert, mean, coef, near):
    cols = STEP_TILES * 32
    steps = pert.shape[1] // cols
    return pl.pallas_call(
        interp_kernel,
        out_shape=jax.ShapeDtypeStruct(pert.shape, jnp.bfloat16),
        grid_spec=pltpu.PrefetchScalarGridSpec(
            num_scalar_prefetch=1,
            grid=(steps,),
            in_specs=[
                pl.BlockSpec((8, cols, 256), lambda i, *_: (0, i, 0)),
                pl.BlockSpec((8, cols), lambda i, *_: (0, i)),
                pl.BlockSpec((4, cols), lambda i, *_: (0, i)),
                pl.BlockSpec((36, 256, 256), lambda i, *_: (0, 0, 0), pipeline_mode=pl.Buffered(1)),
            ],
            out_specs=pl.BlockSpec((8, cols, 256), lambda i, *_: (0, i, 0)),
        ),
        compiler_params=pltpu.CompilerParams(
            dimension_semantics=("arbitrary",), vmem_limit_bytes=58 << 20),
        name="interp",
    )(position, pert, mean, coef, near)


def local(
    obs_pert, obs_dep, valid_rows, local_lists, state_mean, state_pert, interp_lists, interp_coef
):
    n_lon = lax.axis_size("lon")
    domains_here = local_lists.shape[0]
    tile = jnp.concatenate([
        jnp.pad(local_lists, ((0, 0), (0, 128 - local_lists.shape[1])), constant_values=-1),
        jnp.pad(valid_rows[None, :], ((0, 3), (0, 64))),
    ], axis=0)
    near = near_weights(tile, obs_pert, obs_dep)
    owner = interp_lists // domains_here
    within = interp_lists % domains_here
    lat_step = owner // n_lon - lax.axis_index("lat")
    lon_step = (owner % n_lon - lax.axis_index("lon") + 1) % n_lon - 1
    position = ((lat_step + 1) * 3 + lon_step + 1) * domains_here + within
    return interpolate(position.reshape(-1), state_pert, state_mean, interp_coef, near.reshape(36, 256, 256))


def solution(mesh):
    in_specs = (
        P(("lat", "lon"), None, None),
        P(("lat", "lon"), None),
        P(("lat", "lon")),
        P(("lat", "lon"), None),
        P(None, ("lat", "lon")),
        P(None, ("lat", "lon"), None),
        P(("lat", "lon"), None),
        P(None, ("lat", "lon")),
    )
    out_specs = P(None, ("lat", "lon"), None)
    return jax.shard_map(local, mesh=mesh, in_specs=in_specs, out_specs=out_specs, check_vma=False)
```

time: 176 us -> 155 us (0.88)
  Pallas kernels: 168 us -> 151 us
  local copies, waits for them, and re-layouts: 3.17 us -> 0.77 us
    pallas_call x1, Pallas kernels: 29.9 us -> 20.1 us  [interpolate(): pl.pallas_call(interp_kernel, out_shape=jax.ShapeDtypeStruct(pert.shape,...]
    pallas_call x2 -> x1, Pallas kernels: 138 us -> 131 us  [near_weights(): pl.pallas_call(reduce_kernel, out_shape=jax.ShapeDtypeStruct((72, 128, 25...]
where the time goes in v4:
time: 155 us; the launch traced here: 154 us
  Pallas kernels  151 us (97%)
  other arithmetic  2.01 us (1%)
    pallas_call x1, Pallas kernels, near_weights(): pl.pallas_call(reduce_kernel, out_shape=jax.ShapeDtypeStruct((72, 128, 25...  131 us
    pallas_call x1, Pallas kernels, interpolate(): pl.pallas_call(interp_kernel, out_shape=jax.ShapeDtypeStruct(pert.shape,...  20.1 us

profile of v4, /device:TPU:1, one launch (start us, length us, event | category | flops | bytes accessed | tf_op | source)
XLA Modules:
  0.0 154.0 jit_solution(14829670640223880467)
XLA Ops:
  0.0 0.7 fusion.9
  0.7 1.3 pad_add_fusion.tile_ref
  2.0 0.1 copy.9
  2.1 0.7 reshape.6.pos_ref
  2.8 131.0 %reduce.1 = bf16[72,128,256]{2,1,0:T(8,128)(2,1)} custom-call(s32[8,128]{1,0:T(8,128)} %pad_add_fusion.tile_ref, bf16[64,128,256]{2,1,0:T(8,128)(2,1)} %pert_ref.2, bf16[64,128]{1,0:T(8,128)(2,1)} %dep_ref.1), custom_call_target="tpu_custom_call" | custom-call | tf_op jit(solution)/shard_map/reduce/pallas_call | solution.py:468
  133.8 20.1 %interp.1 = bf16[8,2048,256]{2,1,0:T(8,128)(2,1)} custom-call(s32[256]{0:T(256)} %reshape.6.pos_ref, bf16[8,2048,256]{2,1,0:T(8,128)(2,1)} %pert_ref.3, f32[8,2048]{1,0:T(8,128)} %mean_ref.1, f32[4,2048]{1,0:T(4,128)} %coef_ref.1, bf16[36,256,256]{2,1,0:T(8,128)(2,1)} %bitcast.2), custom_call_target="tpu_custom_call" | custom-call | tf_op jit(solution)/shard_map/interp/pallas_call | solution.py:507

commit v5 on v4

--- a/solution.py
+++ b/solution.py
@@ -177,14 +177,14 @@
     tiles[2 * k + 1, :, right] = (t22 + second).astype(jnp.bfloat16)
 
 
-def reduce_kernel(tile_ref, pert_ref, dep_ref, out_ref, *scratch):
+def reduce_kernel(lists_ref, rows_ref, pert_ref, dep_ref, out_ref, *scratch):
     n = len(PARTS)
     scratch = list(scratch)
 
     def take(count):
         taken, scratch[:count] = scratch[:count], []
         return taken
-    held, keys_vmem, keys_ref, valid_ref, sib_tile, sib_dep, blocks, deps, near, fin, fin_extra = take(11)
+    tile_ref, held, keys_vmem, keys_ref, valid_ref, sib_tile, sib_dep, blocks, deps, near, fin, fin_extra = take(12)
     grams = take(n)
     bufs = [[take(6) for _ in range(n)] for _ in range(2)] + [[take(3) for _ in range(n)]]
     send_sem, recv_sem, load_sem, list_send, list_recv, sib_send, sib_recv, halo_send, halo_recv, out_sem = scratch
@@ -197,6 +197,9 @@
     sibling = shifted(pos, "c", 1)
     load = pltpu.make_async_copy(pert_ref, blocks.at[pl.ds(0, 64)], load_sem.at[0])
     load.start()
+    tile_ref[...] = jnp.full((8, 128), -1, jnp.int32)
+    tile_ref[pl.ds(0, 4), pl.ds(0, 24)] = lists_ref[...]
+    tile_ref[pl.ds(4, 1), pl.ds(0, 64)] = rows_ref[...]
     own_valid = pltpu.make_async_copy(tile_ref, valid_ref.at[0], load_sem.at[1])
     own_valid.start()
     me = (y * 4 + x) * 4 + z
@@ -329,10 +332,13 @@
             fin_extra[...] = total
 
     def fill(count, place):
+        together = 3 if count % 3 == 0 else 2
+
         def step(j, carry):
-            fill_server(tuple(at % 4 for at in place(j)), keys_ref, valid_ref, blocks, deps, grams)
+            for k in range(together):
+                fill_server(tuple(at % 4 for at in place(j * together + k)), keys_ref, valid_ref, blocks, deps, grams)
             return carry
-        lax.fori_loop(0, count, step, 0)
+        lax.fori_loop(0, count // together, step, 0)
 
     fill(8, lambda j: (x + 2, j // 4, z + j))
     send_far(0, 0, (0,))
@@ -437,7 +443,7 @@
         copy.wait()
 
 
-def near_weights(tile, pert, dep):
+def near_weights(lists, rows, pert, dep):
     n = len(PARTS)
     hbm = pl.BlockSpec(memory_space=pltpu.HBM)
     full = pl.BlockSpec(memory_space=pltpu.VMEM)
@@ -445,6 +451,7 @@
     def vmem(shape, kind):
         return pltpu.VMEM(shape, kind)
     scratch = [
+        vmem((8, 128), jnp.int32),
         vmem((64, 8, 128), jnp.int32),
         vmem((64, 128), jnp.int32),
         pltpu.SMEM((64, 128), jnp.int32),
@@ -468,78 +475,101 @@
     return pl.pallas_call(
         reduce_kernel,
         out_shape=jax.ShapeDtypeStruct((72, 128, 256), jnp.bfloat16),
-        in_specs=[full, hbm, full],
+        in_specs=[full, full, hbm, full],
         out_specs=hbm,
         scratch_shapes=scratch,
         compiler_params=pltpu.CompilerParams(
             collective_id=1, has_side_effects=True, vmem_limit_bytes=58 << 20),
         name="reduce",
-    )(tile, pert, dep)
-
-
-STEP_TILES = 4
-
-
-def interp_kernel(pos_ref, pert_ref, mean_ref, coef_ref, near_ref, out_ref):
-    step = pl.program_id(0)
-    mean_cols = mean_ref[...].T
-    coef = coef_ref[...]
-    coef_cols = jnp.concatenate([coef, coef], axis=0).T
-    for tile in range(STEP_TILES):
-        span = pl.ds(tile * 32, 32)
-        held = pert_ref[:, span, :].reshape(256, 256)
-        total = None
-        for pair in ((0, 1), (2, 3)):
-            near = [near_ref[pos_ref[(step * STEP_TILES + tile) * 4 + corner]] for corner in pair]
-            both = jnp.dot(held, jnp.concatenate(near, axis=1), preferred_element_type=jnp.float32)
-            for k, corner in enumerate(pair):
+    )(lists, rows, pert, dep)
+
+
+CHUNK = 256
+
+
+def interp_kernel(lists_ref, mean_ref, coef_ref, pert_ref, near_ref, out_ref, held, near, done, near_sem, in_sem, out_sem):
+    chunks = held.shape[1] // CHUNK
+    a, b = lax.axis_index("lat"), lax.axis_index("lon")
+    fetch_near = [pltpu.make_async_copy(near_ref.at[pl.ds(9 * k, 9)], near.at[pl.ds(9 * k, 9)], near_sem.at[k])
+                  for k in range(4)]
+    for copy in fetch_near:
+        copy.start()
+
+    def place(tile, corner):
+        domain = lists_ref[corner, tile]
+        lat, lon = domain // 64, (domain // 4) % 16
+        return ((lat - a + 1) * 3 + (lon - b + 17) % 16) * 4 + domain % 4
+
+    def fetch(c):
+        span = pl.ds(pl.multiple_of(c * CHUNK, CHUNK), CHUNK)
+        return pltpu.make_async_copy(pert_ref.at[:, span], held.at[:, span], in_sem.at[c])
+
+    def write(c):
+        span = pl.ds(pl.multiple_of(c * CHUNK, CHUNK), CHUNK)
+        return pltpu.make_async_copy(done.at[:, span], out_ref.at[:, span], out_sem.at[c])
+
+    for c in range(2):
+        fetch(c).start()
+    for copy in fetch_near:
+        copy.wait()
+
+    @pl.loop(2, chunks)
+    def _(c):
+        fetch(c).start()
+
+    @pl.loop(0, chunks)
+    def _(c):
+        first = pl.multiple_of(c * CHUNK, CHUNK)
+        mean_cols = mean_ref[:, pl.ds(first, CHUNK)].T
+        coef = coef_ref[:, pl.ds(first, CHUNK)]
+        coef_cols = jnp.concatenate([coef, coef], axis=0).T
+        fetch(c).wait()
+        for tile in range(CHUNK // 32):
+            span = pl.ds(pl.multiple_of(first + tile * 32, 32), 32)
+            left = held[:, span, :].reshape(256, 256)
+            total = None
+            for corner in range(4):
+                prod = jnp.dot(left, near[place(c * (CHUNK // 32) + tile, corner)], preferred_element_type=jnp.float32)
                 factor = coef_cols[tile * 32:tile * 32 + 32, corner:corner + 1]
-                term = both[:, 256 * k:256 * k + 256].reshape(8, 32, 256) * factor[None]
+                term = prod.reshape(8, 32, 256) * factor[None]
                 total = term if total is None else total + term
-        for level in range(8):
-            base = mean_cols[tile * 32:tile * 32 + 32, level:level + 1]
-            out_ref[level, span, :] = (total[level] + base).astype(jnp.bfloat16)
-
-
-def interpolate(position, pert, mean, coef, near):
-    cols = STEP_TILES * 32
-    steps = pert.shape[1] // cols
+            for level in range(8):
+                base = mean_cols[tile * 32:tile * 32 + 32, level:level + 1]
+                done[level, span, :] = (total[level] + base).astype(jnp.bfloat16)
+        write(c).start()
+
+    @pl.loop(0, chunks)
+    def _(c):
+        write(c).wait()
+
+
+def interpolate(lists, pert, mean, coef, near):
+    hbm = pl.BlockSpec(memory_space=pltpu.HBM)
+    full = pl.BlockSpec(memory_space=pltpu.VMEM)
+    chunks = pert.shape[1] // CHUNK
     return pl.pallas_call(
         interp_kernel,
         out_shape=jax.ShapeDtypeStruct(pert.shape, jnp.bfloat16),
-        grid_spec=pltpu.PrefetchScalarGridSpec(
-            num_scalar_prefetch=1,
-            grid=(steps,),
-            in_specs=[
-                pl.BlockSpec((8, cols, 256), lambda i, *_: (0, i, 0)),
-                pl.BlockSpec((8, cols), lambda i, *_: (0, i)),
-                pl.BlockSpec((4, cols), lambda i, *_: (0, i)),
-                pl.BlockSpec((36, 256, 256), lambda i, *_: (0, 0, 0), pipeline_mode=pl.Buffered(1)),
-            ],
-            out_specs=pl.BlockSpec((8, cols, 256), lambda i, *_: (0, i, 0)),
-        ),
-        compiler_params=pltpu.CompilerParams(
-            dimension_semantics=("arbitrary",), vmem_limit_bytes=58 << 20),
+        in_specs=[pl.BlockSpec(memory_space=pltpu.SMEM), full, full, hbm, hbm],
+        out_specs=hbm,
+        scratch_shapes=[
+            pltpu.VMEM(pert.shape, jnp.bfloat16),
+            pltpu.VMEM(near.shape, jnp.bfloat16),
+            pltpu.VMEM(pert.shape, jnp.bfloat16),
+            pltpu.SemaphoreType.DMA((4,)),
+            pltpu.SemaphoreType.DMA((chunks,)),
+            pltpu.SemaphoreType.DMA((chunks,)),
+        ],
+        compiler_params=pltpu.CompilerParams(vmem_limit_bytes=58 << 20),
         name="interp",
-    )(position, pert, mean, coef, near)
+    )(lists, mean, coef, pert, near)
 
 
 def local(
     obs_pert, obs_dep, valid_rows, local_lists, state_mean, state_pert, interp_lists, interp_coef
 ):
-    n_lon = lax.axis_size("lon")
-    domains_here = local_lists.shape[0]
-    tile = jnp.concatenate([
-        jnp.pad(local_lists, ((0, 0), (0, 128 - local_lists.shape[1])), constant_values=-1),
-        jnp.pad(valid_rows[None, :], ((0, 3), (0, 64))),
-    ], axis=0)
-    near = near_weights(tile, obs_pert, obs_dep)
-    owner = interp_lists // domains_here
-    within = interp_lists % domains_here
-    lat_step = owner // n_lon - lax.axis_index("lat")
-    lon_step = (owner % n_lon - lax.axis_index("lon") + 1) % n_lon - 1
-    position = ((lat_step + 1) * 3 + lon_step + 1) * domains_here + within
-    return interpolate(position.reshape(-1), state_pert, state_mean, interp_coef, near.reshape(36, 256, 256))
+    near = near_weights(local_lists, valid_rows[None, :], obs_pert, obs_dep)
+    return interpolate(interp_lists.T, state_pert, state_mean, interp_coef, near.reshape(36, 256, 256))
 
 
 def solution(mesh):

time: 155 us -> 142 us (0.916)
  Pallas kernels: 151 us -> 142 us
  other arithmetic: 2.01 us -> 0 us
    pallas_call x1, Pallas kernels: 131 us -> 125 us  [near_weights(): pl.pallas_call(reduce_kernel, out_shape=jax.ShapeDtypeStruct((72, 128, 25...]
    pallas_call x1, Pallas kernels: 20.1 us -> 16.2 us  [interpolate(): pl.pallas_call(interp_kernel, out_shape=jax.ShapeDtypeStruct(pert.shape,...]
where the time goes in v5:
time: 142 us
  Pallas kernels  142 us (100%)
    pallas_call x1, Pallas kernels, near_weights(): pl.pallas_call(reduce_kernel, out_shape=jax.ShapeDtypeStruct((72, 128, 25...  125 us
    pallas_call x1, Pallas kernels, interpolate(): pl.pallas_call(interp_kernel, out_shape=jax.ShapeDtypeStruct(pert.shape,...  16.2 us

profile of v5, /device:TPU:1, one launch (start us, length us, event | category | flops | bytes accessed | tf_op | source)
XLA Modules:
  0.0 141.8 jit_solution(7047733224654338069)
XLA Ops:
  0.0 125.4 %reduce.1 = bf16[72,128,256]{2,1,0:T(8,128)(2,1)} custom-call(s32[4,24]{1,0:T(4,128)} %lists_ref.1, s32[1,64]{1,0:T(1,128)} %bitcast.5, bf16[64,128,256]{2,1,0:T(8,128)(2,1)} %pert_ref.2, bf16[64,128]{1,0:T(8,128)(2,1)} %dep_ref.1), custom_call_target="tpu_custom_call" | custom-call | tf_op jit(solution)/shard_map/reduce/pallas_call | solution.py:475
  125.4 16.2 %interp.1 = bf16[8,2048,256]{2,1,0:T(8,128)(2,1)} custom-call(s32[4,64]{1,0:T(4,128)} %bitcast.4, f32[8,2048]{1,0:T(8,128)} %mean_ref.1, f32[4,2048]{1,0:T(4,128)} %coef_ref.1, bf16[8,2048,256]{2,1,0:T(8,128)(2,1)} %pert_ref.3, bf16[36,256,256]{2,1,0:T(8,128)(2,1)} %bitcast.3), custom_call_target="tpu_custom_call" | custom-call | tf_op jit(solution)/shard_map/interp/pallas_call | solution.py:550

commit v6 on v5

--- a/solution.py
+++ b/solution.py
@@ -12,6 +12,7 @@
 BIG = 1 << 20
 PARTS = ((400, jnp.bfloat16, "xyz"), (352, jnp.bfloat16, "yzx"), (272, jnp.bfloat16, "zxy"), (16, jnp.float32, "zxy"))
 STARTS = (0, 400, 752)
+SPANS = ((0, 2), (2, 1), (3, 1))
 
 
 def coords():
@@ -143,18 +144,17 @@
 
 def listed_keys(held, own, other):
     lane = lax.broadcasted_iota(jnp.int32, (64, 128), 1)
-    values = []
-    for dom in range(4):
-        entry = held[:, dom, :]
-        owner, local_index = entry >> 6, entry & 63
-        block = jnp.where(owner == own, local_index, local_index + 64)
-        values.append(jnp.where((owner == own) | (owner == other), dom * 4096 + lane * 128 + block, BIG))
+    dom = lane // 24
+    entry = held[:, 0, :]
+    owner, local_index = entry >> 6, entry & 63
+    block = jnp.where(owner == own, local_index, local_index + 64)
+    mine = ((owner == own) | (owner == other)) & (lane < 96)
+    value = jnp.where(mine, dom * 4096 + (lane - 24 * dom) * 128 + block, BIG)
     out = jnp.full((64, 128), BIG, jnp.int32)
     for k in range(4):
-        least = functools.reduce(jnp.minimum, values)
-        least = jnp.min(least, axis=1, keepdims=True)
+        least = jnp.min(value, axis=1, keepdims=True)
         out = jnp.where(lane == k, least, out)
-        values = [jnp.where(value > least, value, BIG) for value in values]
+        value = jnp.where(value > least, value, BIG)
     return out
 
 
@@ -165,15 +165,14 @@
     packed = packed_ref[index + (pl.ds(128, 128),)].astype(jnp.float32)
     rest = packed_ref[index + (pl.ds(256, 16),)].astype(jnp.float32)
     rest = rest[:4] + rest[4:8]
-    columns = jnp.concatenate([rest, rest], axis=0).T
-    first, second = columns[:, 2:3], columns[:, 3:4]
+    first, second = rest[2:3], rest[3:4]
     turned = packed.T
     t11 = jnp.where(col > row, packed, jnp.where(col == row, rest[0:1], turned))
     t22 = jnp.where(col < row, packed, jnp.where(col == row, rest[1:2], turned))
     left, right = pl.ds(0, 128), pl.ds(128, 128)
     tiles[2 * k, :, left] = (t11 + first).astype(jnp.bfloat16)
-    tiles[2 * k, :, right] = (wide + first).astype(jnp.bfloat16)
-    tiles[2 * k + 1, :, left] = (wide.T + second).astype(jnp.bfloat16)
+    tiles[2 * k, :, right] = (wide + second).astype(jnp.bfloat16)
+    tiles[2 * k + 1, :, left] = (wide.T + first).astype(jnp.bfloat16)
     tiles[2 * k + 1, :, right] = (t22 + second).astype(jnp.bfloat16)
 
 
@@ -197,13 +196,17 @@
     sibling = shifted(pos, "c", 1)
     load = pltpu.make_async_copy(pert_ref, blocks.at[pl.ds(0, 64)], load_sem.at[0])
     load.start()
-    tile_ref[...] = jnp.full((8, 128), -1, jnp.int32)
+    tile_ref[...] = jnp.zeros((8, 128), jnp.int32)
     tile_ref[pl.ds(0, 4), pl.ds(0, 24)] = lists_ref[...]
     tile_ref[pl.ds(4, 1), pl.ds(0, 64)] = rows_ref[...]
     own_valid = pltpu.make_async_copy(tile_ref, valid_ref.at[0], load_sem.at[1])
     own_valid.start()
     me = (y * 4 + x) * 4 + z
-    held[me] = tile_ref[...]
+    entries = tile_ref[...]
+    listed = entries
+    for d in range(1, 4):
+        listed = listed + pltpu.roll(jnp.roll(entries, -d, 0), 24 * d, 1)
+    held[me] = listed[0:1]
     deps[pl.ds(0, 64)] = dep_ref[...].astype(jnp.float32)
     greet([shifted(pos, axis, step) for axis in "zxy" for step in (1, 2, 3)]
           + [sibling, lat_up, lat_down, lon_up, lon_down])
@@ -389,7 +392,7 @@
     halos = {}
 
     def halo(chunk, k, origin, to, target):
-        span = pl.ds(2 * chunk, 2)
+        span = pl.ds(*SPANS[chunk])
         copy = pltpu.make_async_remote_copy(
             src_ref=near.at[origin + (span,)], dst_ref=near.at[to + (span,)],
             send_sem=halo_send.at[chunk, k], recv_sem=halo_recv.at[chunk, k],
@@ -401,11 +404,12 @@
     outs = []
 
     def unpack(chunk, at):
-        first = (at[0] * 3 + at[1]) * 4 + 2 * chunk
-        for k in range(2):
-            full_weights(near, at + (2 * chunk + k,), blocks, first + k)
-        copy = pltpu.make_async_copy(
-            blocks.at[pl.ds(2 * first, 4)], out_ref.at[pl.ds(2 * first, 4)], out_sem.at[len(outs)])
+        start_dom, count = SPANS[chunk]
+        first = (at[0] * 3 + at[1]) * 4 + start_dom
+        for k in range(count):
+            full_weights(near, at + (start_dom + k,), blocks, first + k)
+        span = pl.ds(2 * first, 2 * count)
+        copy = pltpu.make_async_copy(blocks.at[span], out_ref.at[span], out_sem.at[len(outs)])
         copy.start()
         outs.append(copy)
 
@@ -425,14 +429,16 @@
     own_halo(0)
     solve((2, 3), lambda: corner_halo(0))
     own_halo(1)
-    for chunk in range(2):
+    own_halo(2)
+    for chunk in range(3):
         unpack(chunk, (1, 1))
     for column in (0, 2):
         unpack(0, (1, column))
-    corner_halo(1)
-    for column in (0, 2):
-        unpack(1, (1, column))
-    for chunk in range(2):
+    for chunk in (1, 2):
+        corner_halo(chunk)
+        for column in (0, 2):
+            unpack(chunk, (1, column))
+    for chunk in range(3):
         for column in (1, 0, 2):
             for line in (0, 2):
                 halos[chunk, (line, column)].wait_recv()
@@ -452,7 +458,7 @@
         return pltpu.VMEM(shape, kind)
     scratch = [
         vmem((8, 128), jnp.int32),
-        vmem((64, 8, 128), jnp.int32),
+        vmem((64, 1, 128), jnp.int32),
         vmem((64, 128), jnp.int32),
         pltpu.SMEM((64, 128), jnp.int32),
         pltpu.SMEM((2, 8, 128), jnp.int32),
@@ -471,7 +477,7 @@
     for r, t, _ in PARTS:
         scratch += [vmem((r, 128), t)] * 3
     scratch += [pltpu.SemaphoreType.DMA(shape) for shape in (
-        (3, n, 6), (3, n, 6), (4,), (3, 3), (3, 3), (3,), (3,), (2, 8), (2, 8), (18,))]
+        (3, n, 6), (3, n, 6), (4,), (3, 3), (3, 3), (3,), (3,), (3, 8), (3, 8), (27,))]
     return pl.pallas_call(
         reduce_kernel,
         out_shape=jax.ShapeDtypeStruct((72, 128, 256), jnp.bfloat16),
@@ -520,22 +526,29 @@
     @pl.loop(0, chunks)
     def _(c):
         first = pl.multiple_of(c * CHUNK, CHUNK)
-        mean_cols = mean_ref[:, pl.ds(first, CHUNK)].T
-        coef = coef_ref[:, pl.ds(first, CHUNK)]
-        coef_cols = jnp.concatenate([coef, coef], axis=0).T
         fetch(c).wait()
+        lane = lax.broadcasted_iota(jnp.int32, (8, 128), 1)
+        level = lax.broadcasted_iota(jnp.int32, (8, 128), 0)
+
+        def spread(value, group):
+            value = jnp.where(lane // 32 == group, value, 0.0)
+            value = value + pltpu.roll(value, 32, 1)
+            return value + pltpu.roll(value, 64, 1)
+
         for tile in range(CHUNK // 32):
             span = pl.ds(pl.multiple_of(first + tile * 32, 32), 32)
-            left = held[:, span, :].reshape(256, 256)
-            total = None
+            lanes = pl.ds(pl.multiple_of(first + tile // 4 * 128, 128), 128)
+            means = spread(mean_ref[:, lanes], tile % 4)
+            coef = coef_ref[:, lanes]
+            coefs = spread(jnp.concatenate([coef, coef], axis=0), tile % 4)
+            total = jnp.concatenate(
+                [jnp.sum(jnp.where(level == lane // 32 + 4 * k, means, 0.0), axis=0, keepdims=True) for k in range(2)], axis=1)
+            right = held[:, span, :].reshape(256, 256)
             for corner in range(4):
-                prod = jnp.dot(left, near[place(c * (CHUNK // 32) + tile, corner)], preferred_element_type=jnp.float32)
-                factor = coef_cols[tile * 32:tile * 32 + 32, corner:corner + 1]
-                term = prod.reshape(8, 32, 256) * factor[None]
-                total = term if total is None else total + term
-            for level in range(8):
-                base = mean_cols[tile * 32:tile * 32 + 32, level:level + 1]
-                done[level, span, :] = (total[level] + base).astype(jnp.bfloat16)
+                prod = lax.dot_general(near[place(c * (CHUNK // 32) + tile, corner)], right, (((1,), (1,)), ((), ())), preferred_element_type=jnp.float32)
+                row = coefs[corner:corner + 1]
+                total = total + prod * jnp.concatenate([row, row], axis=1)
+            done[:, span, :] = total.astype(jnp.bfloat16).T.reshape(8, 32, 256)
         write(c).start()
 
     @pl.loop(0, chunks)

time: 142 us -> 139 us (0.979)
  Pallas kernels: 142 us -> 138 us
    pallas_call x1, Pallas kernels: 125 us -> 123 us  [near_weights(): pl.pallas_call(reduce_kernel, out_shape=jax.ShapeDtypeStruct((72, 128, 25...]
where the time goes in v6:
time: 139 us
  Pallas kernels  138 us (99%)
    pallas_call x1, Pallas kernels, near_weights(): pl.pallas_call(reduce_kernel, out_shape=jax.ShapeDtypeStruct((72, 128, 25...  123 us
    pallas_call x1, Pallas kernels, interpolate(): pl.pallas_call(interp_kernel, out_shape=jax.ShapeDtypeStruct(pert.shape,...  15.5 us

profile of v6, /device:TPU:1, one launch (start us, length us, event | category | flops | bytes accessed | tf_op | source)
XLA Modules:
  0.0 138.6 jit_solution(6674731044532171631)
XLA Ops:
  0.0 122.9 %reduce.1 = bf16[72,128,256]{2,1,0:T(8,128)(2,1)} custom-call(s32[4,24]{1,0:T(4,128)} %lists_ref.1, s32[1,64]{1,0:T(1,128)} %bitcast.5, bf16[64,128,256]{2,1,0:T(8,128)(2,1)} %pert_ref.2, bf16[64,128]{1,0:T(8,128)(2,1)} %dep_ref.1), custom_call_target="tpu_custom_call" | custom-call | tf_op jit(solution)/shard_map/reduce/pallas_call | solution.py:481
  122.9 15.5 %interp.1 = bf16[8,2048,256]{2,1,0:T(8,128)(2,1)} custom-call(s32[4,64]{1,0:T(4,128)} %bitcast.4, f32[8,2048]{1,0:T(8,128)} %mean_ref.1, f32[4,2048]{1,0:T(4,128)} %coef_ref.1, bf16[8,2048,256]{2,1,0:T(8,128)(2,1)} %pert_ref.3, bf16[36,256,256]{2,1,0:T(8,128)(2,1)} %bitcast.3), custom_call_target="tpu_custom_call" | custom-call | tf_op jit(solution)/shard_map/interp/pallas_call | solution.py:563

commit v7 on v6

--- a/solution.py
+++ b/solution.py
@@ -185,7 +185,7 @@
         return taken
     tile_ref, held, keys_vmem, keys_ref, valid_ref, sib_tile, sib_dep, blocks, deps, near, fin, fin_extra = take(12)
     grams = take(n)
-    bufs = [[take(6) for _ in range(n)] for _ in range(2)] + [[take(3) for _ in range(n)]]
+    bufs = [[take(4) for _ in range(n)] for _ in range(2)] + [[take(3) for _ in range(n)]]
     send_sem, recv_sem, load_sem, list_send, list_recv, sib_send, sib_recv, halo_send, halo_recv, out_sem = scratch
 
     pos = coords()
@@ -254,9 +254,15 @@
     def half(i, phase, target, upper):
         return prefix(i, phase) + (target, pl.ds(2 * upper, 2))
 
+    def landing(i, phase, k):
+        if k < 2:
+            return bufs[phase][i][k]
+        which, upper = {2: (3, 1), 3: (3, 0), 4: (2, 0), 5: (2, 1)}[k]
+        return bufs[phase][i][which].at[pl.ds(2 * upper, 2)]
+
     def start(i, phase, k, source, to_right):
         copy = pltpu.make_async_remote_copy(
-            src_ref=source, dst_ref=bufs[phase][i][k],
+            src_ref=source, dst_ref=landing(i, phase, k),
             send_sem=send_sem.at[phase, i, k], recv_sem=recv_sem.at[phase, i, k],
             device_id=shifted(pos, PARTS[i][2][phase], 1 if to_right else 3), device_id_type=MESH)
         copy.start()
@@ -298,30 +304,35 @@
             each(phase, body)
             start(i, phase, 4 + k, got, k == 0)
 
-    def finish(i, phase):
-        m = coord(i, phase)
+    def arrived(i, phase):
         for k in (2, 3, 4, 5):
             flights[phase][i][k].wait_recv()
-        for upper, pair in enumerate(((4, 3), (2, 5))):
-            f, g = (bufs[phase][i][k] for k in pair)
-
-            def body(lead, f=f, g=g, upper=upper):
-                index = local_index(i, phase, m, upper, lead)
-                total = grams[i][index].astype(jnp.float32) + f[lead].astype(jnp.float32) + g[lead].astype(jnp.float32)
-                grams[i][index] = total.astype(grams[i].dtype)
-            each(phase, body)
-
-    def send_last(i):
-        copies = []
-        for step in (1, 2, 3):
-            copy = pltpu.make_async_remote_copy(
-                src_ref=grams[i].at[prefix(i, 2) + ((coord(i, 2) + step) % 4,)], dst_ref=bufs[2][i][step - 1],
-                send_sem=send_sem.at[2, i, step - 1], recv_sem=recv_sem.at[2, i, step - 1],
-                device_id=shifted(pos, PARTS[i][2][2], step), device_id_type=MESH)
-            copy.start()
-            copies.append(copy)
-        sends.extend(copies)
-        return copies
+
+    def finish(i, phase, target):
+        pairs, singles = bufs[phase][i][2:]
+
+        def body(lead):
+            index = prefix(i, phase + 1) + lead
+            total = (grams[i][index].astype(jnp.float32) + pairs[lead].astype(jnp.float32)
+                     + singles[lead].astype(jnp.float32))
+            grams[i][index] = total.astype(grams[i].dtype)
+        if phase == 1:
+            body((target,))
+            return
+
+        def step(j, carry):
+            body((target, j))
+            return carry
+        lax.fori_loop(0, 4, step, 0)
+
+    def send_last(i, step):
+        copy = pltpu.make_async_remote_copy(
+            src_ref=grams[i].at[prefix(i, 2) + ((coord(i, 2) + step) % 4,)], dst_ref=bufs[2][i][step - 1],
+            send_sem=send_sem.at[2, i, step - 1], recv_sem=recv_sem.at[2, i, step - 1],
+            device_id=shifted(pos, PARTS[i][2][2], step), device_id_type=MESH)
+        copy.start()
+        sends.append(copy)
+        return copy
 
     def finish_last(i, copies):
         for copy in copies:
@@ -369,16 +380,26 @@
     for i in range(n):
         forward(i, 0)
     for i in range(n):
-        finish(i, 0)
+        arrived(i, 0)
+        m = coord(i, 1)
+        finish(i, 0, (m + 2) % 4)
         send_far(i, 1)
+        finish(i, 0, (m + 1) % 4)
         send_right(i, 1)
+        finish(i, 0, (m + 3) % 4)
         send_left(i, 1)
     for i in range(n):
+        finish(i, 0, coord(i, 1))
         forward(i, 1)
     last = []
     for i in range(n):
-        finish(i, 1)
-        last.append(send_last(i))
+        arrived(i, 1)
+        copies = []
+        for step in (2, 1, 3):
+            finish(i, 1, (coord(i, 2) + step) % 4)
+            copies.append(send_last(i, step))
+        finish(i, 1, coord(i, 2))
+        last.append(copies)
     for i in range(n):
         finish_last(i, last[i])
 
@@ -473,7 +494,7 @@
     scratch += [vmem((4, 4, 4, r, 128), t) for r, t, _ in PARTS]
     for shape in ((2, 4), (2,)):
         for r, t, _ in PARTS:
-            scratch += [vmem(shape + (r, 128), t)] * 6
+            scratch += [vmem(shape + (r, 128), t)] * 2 + [vmem((4,) + shape[1:] + (r, 128), t)] * 2
     for r, t, _ in PARTS:
         scratch += [vmem((r, 128), t)] * 3
     scratch += [pltpu.SemaphoreType.DMA(shape) for shape in (
@@ -496,8 +517,8 @@
 def interp_kernel(lists_ref, mean_ref, coef_ref, pert_ref, near_ref, out_ref, held, near, done, near_sem, in_sem, out_sem):
     chunks = held.shape[1] // CHUNK
     a, b = lax.axis_index("lat"), lax.axis_index("lon")
-    fetch_near = [pltpu.make_async_copy(near_ref.at[pl.ds(9 * k, 9)], near.at[pl.ds(9 * k, 9)], near_sem.at[k])
-                  for k in range(4)]
+    fetch_near = [pltpu.make_async_copy(near_ref.at[pl.ds(4 * k, 4)], near.at[pl.ds(4 * k, 4)], near_sem.at[k])
+                  for k in range(9)]
     for copy in fetch_near:
         copy.start()
 
@@ -569,7 +590,7 @@
             pltpu.VMEM(pert.shape, jnp.bfloat16),
             pltpu.VMEM(near.shape, jnp.bfloat16),
             pltpu.VMEM(pert.shape, jnp.bfloat16),
-            pltpu.SemaphoreType.DMA((4,)),
+            pltpu.SemaphoreType.DMA((9,)),
             pltpu.SemaphoreType.DMA((chunks,)),
             pltpu.SemaphoreType.DMA((chunks,)),
         ],

time: 139 us -> 138 us (level)
  no operation moved by 1% of the time
where the time goes in v7:
time: 138 us
  Pallas kernels  138 us (100%)
    pallas_call x1, Pallas kernels, near_weights(): pl.pallas_call(reduce_kernel, out_shape=jax.ShapeDtypeStruct((72, 128, 25...  122 us
    pallas_call x1, Pallas kernels, interpolate(): pl.pallas_call(interp_kernel, out_shape=jax.ShapeDtypeStruct(pert.shape,...  15.5 us

profile of v7, /device:TPU:1, one launch (start us, length us, event | category | flops | bytes accessed | tf_op | source)
XLA Modules:
  0.0 138.0 jit_solution(6961200561431481243)
XLA Ops:
  0.0 122.3 %reduce.1 = bf16[72,128,256]{2,1,0:T(8,128)(2,1)} custom-call(s32[4,24]{1,0:T(4,128)} %lists_ref.1, s32[1,64]{1,0:T(1,128)} %bitcast.5, bf16[64,128,256]{2,1,0:T(8,128)(2,1)} %pert_ref.2, bf16[64,128]{1,0:T(8,128)(2,1)} %dep_ref.1), custom_call_target="tpu_custom_call" | custom-call | tf_op jit(solution)/shard_map/reduce/pallas_call | solution.py:502
  122.3 15.5 %interp.1 = bf16[8,2048,256]{2,1,0:T(8,128)(2,1)} custom-call(s32[4,64]{1,0:T(4,128)} %bitcast.4, f32[8,2048]{1,0:T(8,128)} %mean_ref.1, f32[4,2048]{1,0:T(4,128)} %coef_ref.1, bf16[8,2048,256]{2,1,0:T(8,128)(2,1)} %pert_ref.3, bf16[36,256,256]{2,1,0:T(8,128)(2,1)} %bitcast.3), custom_call_target="tpu_custom_call" | custom-call | tf_op jit(solution)/shard_map/interp/pallas_call | solution.py:584

commit v8 on v7

--- a/solution.py
+++ b/solution.py
@@ -511,7 +511,7 @@
     )(lists, rows, pert, dep)
 
 
-CHUNK = 256
+CHUNK = 512
 
 
 def interp_kernel(lists_ref, mean_ref, coef_ref, pert_ref, near_ref, out_ref, held, near, done, near_sem, in_sem, out_sem):

time: 138 us -> 138 us (level)
  no operation moved by 1% of the time
where the time goes in v8:
time: 138 us
  Pallas kernels  137 us (99%)
    pallas_call x1, Pallas kernels, near_weights(): pl.pallas_call(reduce_kernel, out_shape=jax.ShapeDtypeStruct((72, 128, 25...  122 us
    pallas_call x1, Pallas kernels, interpolate(): pl.pallas_call(interp_kernel, out_shape=jax.ShapeDtypeStruct(pert.shape,...  15 us

profile of v8, /device:TPU:1, one launch (start us, length us, event | category | flops | bytes accessed | tf_op | source)
XLA Modules:
  0.0 137.5 jit_solution(10859473874405988657)
XLA Ops:
  0.0 122.3 %reduce.1 = bf16[72,128,256]{2,1,0:T(8,128)(2,1)} custom-call(s32[4,24]{1,0:T(4,128)} %lists_ref.1, s32[1,64]{1,0:T(1,128)} %bitcast.5, bf16[64,128,256]{2,1,0:T(8,128)(2,1)} %pert_ref.2, bf16[64,128]{1,0:T(8,128)(2,1)} %dep_ref.1), custom_call_target="tpu_custom_call" | custom-call | tf_op jit(solution)/shard_map/reduce/pallas_call | solution.py:502
  122.3 15.0 %interp.1 = bf16[8,2048,256]{2,1,0:T(8,128)(2,1)} custom-call(s32[4,64]{1,0:T(4,128)} %bitcast.4, f32[8,2048]{1,0:T(8,128)} %mean_ref.1, f32[4,2048]{1,0:T(4,128)} %coef_ref.1, bf16[8,2048,256]{2,1,0:T(8,128)(2,1)} %pert_ref.3, bf16[36,256,256]{2,1,0:T(8,128)(2,1)} %bitcast.3), custom_call_target="tpu_custom_call" | custom-call | tf_op jit(solution)/shard_map/interp/pallas_call | solution.py:584
